TPU v7x, 512 devices: a whole 4x8x8 slice. The times are simulated.
512 devices in a mesh: lat: 16 (over x, y_hi), lon: 32 (over y_lo, z, core).
Axes of the slice: x: 4, y: 8 (y_hi: 4, y_lo: 2; y = y_hi * 2 + y_lo), z: 8, core: 2. Of those that a mesh axis runs over, the one named last changes fastest.
Arguments:
- queries: bfloat16 [256, 384, 512], P('lat', 'lon'), may hold values from -70 to 70
- keys: bfloat16 [256, 384, 512], P('lat', 'lon'), may hold values from -4.5 to 4.5
- values: bfloat16 [256, 384, 512], P('lat', 'lon'), may hold values from -6 to 6
- out_weight: bfloat16 [512, 512], replicated, may hold values from -0.25 to 0.25
- d_out: bfloat16 [256, 384, 512], P('lat', 'lon'), may hold values from -6 to 6
Outputs:
- d_queries: bfloat16 [256, 384, 512], P('lat', 'lon')
- d_keys: bfloat16 [256, 384, 512], P('lat', 'lon')
- d_values: bfloat16 [256, 384, 512], P('lat', 'lon')
- d_weight: bfloat16 [512, 512], replicated
All inputs are finite; a program needn't handle non-finite values.
Results may differ from a plain program's by a relative error of at most 0.0096.
Values may be sent and summed in bfloat16 or wider, within the bound.
A program may use at most 64 MiB of HBM per device.

v0:
```python
import jax
import jax.numpy as jnp
from jax import lax
from jax.sharding import PartitionSpec as P

HEADS = 8
RADIUS = 6


def extended(array, sides, width, wrap):
    for axis, dim in sides:
        count, length = (lax.axis_size(axis), array.shape[dim])
        up = [(i, (i + 1) % count) for i in range(count if wrap else count - 1)]
        down = [(j, i) for i, j in up]
        last = lax.slice_in_dim(array, length - width, length, axis=dim)
        initial = lax.slice_in_dim(array, 0, width, axis=dim)
        before = lax.ppermute(last, axis, up)
        after = lax.ppermute(initial, axis, down)
        array = jnp.concatenate([before, array, after], axis=dim)
    return array


def as_sent(array):
    return jax.tree.map(lambda a: a.astype(jnp.bfloat16) if a.dtype == jnp.float32 else a, array)


def extend_rows(field):
    return extended(field, (("lat", 1),), RADIUS, False)


def extend_cols(field):
    return extended(field, (("lon", 2),), RADIUS, True)


def edge_pair(grads, axis_dim):
    length = grads.shape[axis_dim]
    leading = lax.slice_in_dim(grads, 0, RADIUS, axis=axis_dim)
    trailing = lax.slice_in_dim(grads, length - RADIUS, length, axis=axis_dim)
    return jnp.concatenate([leading, trailing], axis=axis_dim)


def settle(grads, arrived, axis_dim):
    length = grads.shape[axis_dim]
    interior = lax.slice_in_dim(grads, RADIUS, length - RADIUS, axis=axis_dim)
    leftover = length - 3 * RADIUS
    leading = lax.slice_in_dim(arrived, 0, RADIUS, axis=axis_dim)
    trailing = lax.slice_in_dim(arrived, 3 * RADIUS, 4 * RADIUS, axis=axis_dim)
    widths_lead = [(0, 0)] * grads.ndim
    widths_lead[axis_dim] = (0, leftover)
    widths_trail = [(0, 0)] * grads.ndim
    widths_trail[axis_dim] = (leftover, 0)
    return interior + jnp.pad(leading, widths_lead) + jnp.pad(trailing, widths_trail)


def fold_rows(grads):
    arrived = extended(as_sent(edge_pair(grads, 1)), (("lat", 1),), RADIUS, False)
    return settle(grads, arrived, 1)


def fold_cols(grads):
    arrived = extended(
        edge_pair(grads, 2).astype(jnp.bfloat16), (("lon", 2),), RADIUS, True
    ).astype(jnp.float32)
    return settle(grads, arrived, 2)


def to_tiles(strip, tile_side, tile_count):
    width = strip.shape[-1]
    shaped = strip.reshape(tile_side, tile_count, tile_side, width)
    return shaped.transpose(1, 0, 2, 3).reshape(tile_count, tile_side * tile_side, width)


def shards(queries, keys, values, out_weight, d_out):
    rows_dev, cols_dev, width = queries.shape
    n_bands = lax.axis_size("lat")
    n_sectors = lax.axis_size("lon")
    head_dim = width // HEADS
    score_scale = head_dim ** (-0.5)
    all_rows = rows_dev * n_bands
    weight_scale = (all_rows * cols_dev * n_sectors) ** (-0.5)
    tokens_dev = rows_dev * cols_dev
    ext_rows = rows_dev + 2 * RADIUS
    ext_cols = cols_dev + 2 * RADIUS
    tile_side = 4
    patch_side = tile_side + 2 * RADIUS
    patch_size = patch_side * patch_side
    tile_cells = tile_side * tile_side
    tile_count = cols_dev // tile_side
    strip_count = rows_dev // tile_side
    stacked = jnp.stack([keys, values])
    region = extend_cols(extend_rows(stacked))
    band_start = lax.axis_index("lat") * rows_dev
    local_ids = jnp.arange(tile_side, dtype=jnp.int32)
    patch_ids = jnp.arange(patch_side, dtype=jnp.int32)
    near = (patch_ids[None, :] >= local_ids[:, None]) & (
        patch_ids[None, :] <= local_ids[:, None] + 2 * RADIUS
    )
    tile_mask = (near[:, None, :, None] & near[None, :, None, :]).reshape(tile_cells, patch_size)
    upstream = d_out.reshape(tokens_dev, width)
    mixed_grad = lax.dot_general(
        upstream, out_weight, (((1,), (1,)), ((), ())), preferred_element_type=jnp.float32
    ).astype(jnp.bfloat16)
    mixed_field = mixed_grad.reshape(rows_dev, cols_dev, width)

    def strip_step(grad_region, strip):
        first_row = strip * tile_side
        query_tiles = to_tiles(
            lax.dynamic_slice_in_dim(queries, first_row, tile_side, 0), tile_side, tile_count
        )
        grad_tiles = to_tiles(
            lax.dynamic_slice_in_dim(mixed_field, first_row, tile_side, 0), tile_side, tile_count
        )
        band_patch = lax.dynamic_slice_in_dim(region, first_row, patch_side, 1)
        patches = jnp.stack(
            [
                band_patch[:, :, t * tile_side : t * tile_side + patch_side]
                for t in range(tile_count)
            ]
        )
        patches = patches.reshape(tile_count, 2, patch_size, HEADS, head_dim)
        key_part = patches[:, 0]
        value_part = patches[:, 1]
        query_part = query_tiles.reshape(tile_count, tile_cells, HEADS, head_dim)
        grad_part = grad_tiles.reshape(tile_count, tile_cells, HEADS, head_dim)
        global_rows = band_start + first_row + patch_ids - RADIUS
        row_valid = (global_rows >= 0) & (global_rows < all_rows)
        cell_valid = jnp.broadcast_to(row_valid[:, None], (patch_side, patch_side)).reshape(
            patch_size
        )
        mask = (tile_mask & cell_valid[None, :])[None, None]
        scores = (
            jnp.einsum("tnhd,tmhd->thnm", query_part, key_part, preferred_element_type=jnp.float32)
            * score_scale
        )
        scores = jnp.where(mask, scores, -1e30)
        peak = jnp.max(scores, axis=-1, keepdims=True)
        lifted = jnp.where(mask, jnp.exp(scores - peak), 0.0)
        probs_full = lifted / jnp.sum(lifted, axis=-1, keepdims=True)
        soft_half = probs_full.astype(jnp.bfloat16)
        att_full = jnp.einsum(
            "thnm,tmhd->tnhd", soft_half, value_part, preferred_element_type=jnp.float32
        )
        row_delta = jnp.sum(grad_part.astype(jnp.float32) * att_full, axis=-1)
        d_prob = jnp.einsum(
            "tnhd,tmhd->thnm", grad_part, value_part, preferred_element_type=jnp.float32
        )
        d_score = (
            probs_full * (d_prob - row_delta.transpose(0, 2, 1)[..., None]) * score_scale
        ).astype(jnp.bfloat16)
        dq_tiles = jnp.einsum(
            "thnm,tmhd->tnhd", d_score, key_part, preferred_element_type=jnp.float32
        )
        dk_tiles = jnp.einsum(
            "thnm,tnhd->tmhd", d_score, query_part, preferred_element_type=jnp.float32
        )
        dv_tiles = jnp.einsum(
            "thnm,tnhd->tmhd", soft_half, grad_part, preferred_element_type=jnp.float32
        )
        both = jnp.stack([dk_tiles, dv_tiles], axis=1).reshape(
            tile_count, 2, patch_side, patch_side, width
        )
        strip_grad = jnp.zeros((2, patch_side, ext_cols, width), jnp.float32)
        for t in range(tile_count):
            left = t * tile_side
            strip_grad = strip_grad + jnp.pad(
                both[t], ((0, 0), (0, 0), (left, ext_cols - left - patch_side), (0, 0))
            )
        current = lax.dynamic_slice_in_dim(grad_region, first_row, patch_side, 1)
        grad_region = lax.dynamic_update_slice_in_dim(
            grad_region, current + strip_grad, first_row, 1
        )
        outputs = (
            att_full.reshape(tile_count, tile_cells, width),
            dq_tiles.reshape(tile_count, tile_cells, width),
        )
        return (grad_region, outputs)

    grad_start = jnp.zeros((2, ext_rows, ext_cols, width), jnp.float32)
    grads, (att_all, dq_all) = lax.scan(
        strip_step, grad_start, jnp.arange(strip_count, dtype=jnp.int32)
    )

    def from_tiles(tiles):
        shaped = tiles.reshape(strip_count, tile_count, tile_side, tile_side, width)
        return shaped.transpose(0, 2, 1, 3, 4).reshape(rows_dev, cols_dev, width)

    attended = from_tiles(att_all).reshape(tokens_dev, width).astype(jnp.bfloat16)
    d_queries = from_tiles(dq_all).astype(jnp.bfloat16)
    folded = fold_rows(fold_cols(grads))
    d_keys = folded[0].astype(jnp.bfloat16)
    d_values = folded[1].astype(jnp.bfloat16)
    partial_weight = lax.dot_general(
        attended, upstream, (((0,), (0,)), ((), ())), preferred_element_type=jnp.float32
    )
    total_weight = lax.psum(partial_weight, ("lat", "lon"))
    d_weight = (total_weight * weight_scale).astype(jnp.bfloat16)
    return (d_queries, d_keys, d_values, d_weight)


def solution(mesh):
    placed = (
        P("lat", "lon", None),
        P("lat", "lon", None),
        P("lat", "lon", None),
        P(),
        P("lat", "lon", None),
    )
    return jax.shard_map(
        shards,
        mesh=mesh,
        in_specs=placed,
        out_specs=(P("lat", "lon", None), P("lat", "lon", None), P("lat", "lon", None), P()),
        check_vma=False,
    )
```

profile of v0, /device:TPU:1, one launch (start us, length us, event | category | flops | bytes accessed | tf_op | source)
XLA Modules:
  0.0 533.5 jit_solution(16783759219352668911)
XLA Ops:
  8.6 5.0 collective-permute-start
  16.3 12.3 %collective-permute-done.1 = bf16[2,6,12,512]{3,2,1,0:T(8,128)(2,1)S(1)} collective-permute-done((bf16[2,6,12,512]{3,2,1,0:T(8,128)(2,1)S(1)}, bf16[2,6,12,512]{3,2,1,0:T(8,128)(2,1)S(1)}, u32[]{:S(2)}, u32[]{:S(2)}) %collective-permute-start.1) | collective-permute-done | bytes 147488 | tf_op jit(solution)/shard_map/ppermute | solution.py:18
  29.7 4.5 collective-permute-start.2
  34.2 1.9 collective-permute-start.3
  37.4 2.5 collective-permute-done.2
  39.9 4.1 collective-permute-done.3
  44.0 1.8 pad_maximum_fusion.2
  45.8 2.0 broadcast_in_dim.64.clone
  47.9 173.5 %while.17 = (s32[]{:T(128)}, f32[2,28,24,512]{3,1,2,0:T(8,128)}, bf16[4,3,16,512]{3,2,1,0:T(8,128)(2,1)}, bf16[4,3,16,512]{3,2,1,0:T(8,128)(2,1)}, s32[4]{0:T(12...) while((s32[]{:T(128)}, f32[2,28,24,512]{3,1,2,0:T(8,128)}, ...), condition=%wide.region_4.5_spmd.clone, body=%wide.region_0.4_spmd.clone.sunk | while | flops 80519128 | bytes 63674300 | solution.py:179
  51.7 1.8 constant_dynamic-slice_fusion.11
  58.2 1.6 fusion.59
  62.7 1.8 fusion.61
  64.5 2.0 copy.109
  66.5 1.5 squeeze.45
  68.0 3.1 constant_dynamic-slice_fusion.10
  71.2 2.0 copy.110
  73.2 1.5 squeeze.46
  74.7 2.0 copy.111
  78.2 3.8 copy_add_fusion.2
  82.9 8.3 %dynamic_update_slice.27 = f32[2,28,24,512]{3,1,2,0:T(8,128)} dynamic-update-slice(f32[2,28,24,512]{3,1,2,0:T(8,128)} %get-tuple-element.342, f32[2,16,24,512]{3,1,2,0:T(8,128)S(1)} %copy.112, s32[]{:T(128)} %constant.80.clone.1..sunk, s32[]{:T(128)S(6)} %select_n.40, s32[]{:T(128)} %constant.80.clone.1..sunk, s32[]{:T(128)} %constant.80.clone.1..sunk) | dynamic-update-slice | bytes 3145732 | tf_op jit(solution)/shard_map/while/body/eval_jaxpr/dynamic_update_slice | solution.py:169
  95.1 1.9 constant_dynamic-slice_fusion.11
  101.7 1.6 fusion.59
  106.2 1.8 fusion.61
  108.0 2.0 copy.109
  110.0 1.5 squeeze.45
  111.5 3.1 constant_dynamic-slice_fusion.10
  114.6 2.0 copy.110
  116.7 1.5 squeeze.46
  118.2 2.0 copy.111
  121.7 3.8 copy_add_fusion.2
  126.4 8.3 %dynamic_update_slice.27 = f32[2,28,24,512]{3,1,2,0:T(8,128)} dynamic-update-slice(f32[2,28,24,512]{3,1,2,0:T(8,128)} %get-tuple-element.342, f32[2,16,24,512]{3,1,2,0:T(8,128)S(1)} %copy.112, s32[]{:T(128)} %constant.80.clone.1..sunk, s32[]{:T(128)S(6)} %select_n.40, s32[]{:T(128)} %constant.80.clone.1..sunk, s32[]{:T(128)} %constant.80.clone.1..sunk) | dynamic-update-slice | bytes 3145732 | tf_op jit(solution)/shard_map/while/body/eval_jaxpr/dynamic_update_slice | solution.py:169
  138.5 1.8 constant_dynamic-slice_fusion.11
  145.1 1.6 fusion.59
  149.6 1.8 fusion.61
  151.4 2.0 copy.109
  153.4 1.5 squeeze.45
  154.9 3.1 constant_dynamic-slice_fusion.10
  158.0 2.0 copy.110
  160.0 1.5 squeeze.46
  161.6 2.0 copy.111
  165.1 3.8 copy_add_fusion.2
  169.8 8.2 %dynamic_update_slice.27 = f32[2,28,24,512]{3,1,2,0:T(8,128)} dynamic-update-slice(f32[2,28,24,512]{3,1,2,0:T(8,128)} %get-tuple-element.342, f32[2,16,24,512]{3,1,2,0:T(8,128)S(1)} %copy.112, s32[]{:T(128)} %constant.80.clone.1..sunk, s32[]{:T(128)S(6)} %select_n.40, s32[]{:T(128)} %constant.80.clone.1..sunk, s32[]{:T(128)} %constant.80.clone.1..sunk) | dynamic-update-slice | bytes 3145732 | tf_op jit(solution)/shard_map/while/body/eval_jaxpr/dynamic_update_slice | solution.py:169
  181.8 1.9 constant_dynamic-slice_fusion.11
  188.4 1.6 fusion.59
  192.9 1.8 fusion.61
  194.7 2.0 copy.109
  196.8 1.5 squeeze.45
  198.3 3.1 constant_dynamic-slice_fusion.10
  201.4 2.0 copy.110
  203.4 1.5 squeeze.46
  204.9 2.0 copy.111
  208.5 3.8 copy_add_fusion.2
  213.2 8.2 %dynamic_update_slice.27 = f32[2,28,24,512]{3,1,2,0:T(8,128)} dynamic-update-slice(f32[2,28,24,512]{3,1,2,0:T(8,128)} %get-tuple-element.342, f32[2,16,24,512]{3,1,2,0:T(8,128)S(1)} %copy.112, s32[]{:T(128)} %constant.80.clone.1..sunk, s32[]{:T(128)S(6)} %select_n.40, s32[]{:T(128)} %constant.80.clone.1..sunk, s32[]{:T(128)} %constant.80.clone.1..sunk) | dynamic-update-slice | bytes 3145732 | tf_op jit(solution)/shard_map/while/body/eval_jaxpr/dynamic_update_slice | solution.py:169
  221.4 2.1 convert.16
  223.6 1.9 collective-permute-start.4
  225.5 2.4 collective-permute-start.5
  228.1 2.1 collective-permute-done.4
  230.2 5.1 collective-permute-done.5
  235.8 1.6 copy-done.1
  237.9 4.8 collective-permute-start.6
  246.3 2.4 collective-permute-done.6
  248.7 2.9 collective-permute-done.7
  252.6 271.9 %all-reduce.8.cloned.1.call-done = f32[512,512]{1,0:T(8,128)} async-done(((f32[512,512]{1,0:T(8,128)}), f32[512,512]{1,0:T(8,128)}) %all-reduce.8.cloned.1.call-update) | async-done | bytes 1048592 | tf_op jit(solution)/shard_map/psum | solution.py:195
  524.5 2.1 multiply_convert_fusion
  (180 shorter events, 64.2 us)
Async XLA Ops:
  7.2 28.9 %copy-start = (bf16[512,512]{1,0:T(8,128)(2,1)S(1)}, bf16[512,512]{1,0:T(8,128)(2,1)}, u32[]{:S(2)}) copy-start(bf16[512,512]{1,0:T(8,128)(2,1)} %param.10) | copy-start | bytes 1572868
  7.2 7.8 %copy-start.3 = (bf16[16,12,512]{2,0,1:T(8,128)(2,1)S(1)}, bf16[16,12,512]{2,0,1:T(8,128)(2,1)}, u32[]{:S(2)}) copy-start(bf16[16,12,512]{2,0,1:T(8,128)(2,1)} %param.11) | copy-start | bytes 589828
  7.2 517.3 %all-reduce.8.cloned.1.call-start = ((), (), s32[]{:S(2)}) async-start(), calls=%async_computation | async-start | bytes 2097152 | tf_op jit(solution)/shard_map/psum | solution.py:195
  8.6 7.7 %collective-permute-start = (bf16[2,6,12,512]{3,2,1,0:T(8,128)(2,1)S(1)}, bf16[2,6,12,512]{3,2,1,0:T(8,128)(2,1)S(1)}, u32[]{:S(2)}, u32[]{:S(2)}) collective-permute-start(bf16[2,6,12,512]{3,2,1,0:T(8,128)(2,1)S(1)} %get-tuple-element.231), channel_id=1, source_target_pairs={{0,32},{32,64},{64,96},{96,128},{128,160},{160,192},{192,224},{224... | collective-permute-start | bytes 442376 | tf_op jit(solution)/shard_map/ppermute | solution.py:17
  13.7 14.9 %collective-permute-start.1 = (bf16[2,6,12,512]{3,2,1,0:T(8,128)(2,1)S(1)}, bf16[2,6,12,512]{3,2,1,0:T(8,128)(2,1)S(1)}, u32[]{:S(2)}, u32[]{:S(2)}) collective-permute-start(bf16[2,6,12,512]{3,2,1,0:T(8,128)(2,1)S(1)} %get-tuple-element.232), channel_id=1, source_target_pairs={{32,0},{64,32},{96,64},{128,96},{160,128},{192,160},{224,192},{256... | collective-permute-start | bytes 442376 | tf_op jit(solution)/shard_map/ppermute | solution.py:18
  29.7 10.2 %collective-permute-start.2 = (bf16[2,28,6,512]{3,2,1,0:T(8,128)(2,1)}, bf16[2,28,6,512]{3,2,1,0:T(8,128)(2,1)S(1)}, u32[]{:S(2)}, u32[]{:S(2)}) collective-permute-start(bf16[2,28,6,512]{3,2,1,0:T(8,128)(2,1)} %get-tuple-element.227), channel_id=1, source_target_pairs={{0,1},{1,2},{2,3},{3,4},{4,5},{5,6},{6,7},{7,8},{8,9},{9,10},{10,1... | collective-permute-start | bytes 1032200 | tf_op jit(solution)/shard_map/ppermute | solution.py:17
  34.2 9.8 %collective-permute-start.3 = (bf16[2,28,6,512]{3,2,1,0:T(8,128)(2,1)S(1)}, bf16[2,28,6,512]{3,2,1,0:T(8,128)(2,1)S(1)}, u32[]{:S(2)}, u32[]{:S(2)}) collective-permute-start(bf16[2,28,6,512]{3,2,1,0:T(8,128)(2,1)S(1)} %get-tuple-element.228), channel_id=1, source_target_pairs={{1,0},{2,1},{3,2},{4,3},{5,4},{6,5},{7,6},{8,7},{9,8},{10,9},{11,1... | collective-permute-start | bytes 1032200 | tf_op jit(solution)/shard_map/ppermute | solution.py:18
  58.2 1.6 copy-start.2
  101.7 1.6 copy-start.2
  145.1 1.6 copy-start.2
  188.4 1.6 copy-start.2
  223.5 4.4 copy-start.5
  223.6 6.6 %collective-permute-start.4 = (bf16[2,28,6,512]{3,1,2,0:T(8,128)(2,1)S(1)}, bf16[2,28,6,512]{3,1,2,0:T(8,128)(2,1)S(1)}, u32[]{:S(2)}, u32[]{:S(2)}) collective-permute-start(bf16[2,28,6,512]{3,1,2,0:T(8,128)(2,1)S(1)} %get-tuple-element.225), channel_id=1, source_target_pairs={{0,1},{1,2},{2,3},{3,4},{4,5},{5,6},{6,7},{7,8},{8,9},{9,10},{10,1... | collective-permute-start | bytes 1032200 | tf_op jit(solution)/shard_map/ppermute | solution.py:17
  225.5 9.8 %collective-permute-start.5 = (bf16[2,28,6,512]{3,1,2,0:T(8,128)(2,1)S(1)}, bf16[2,28,6,512]{3,1,2,0:T(8,128)(2,1)S(1)}, u32[]{:S(2)}, u32[]{:S(2)}) collective-permute-start(bf16[2,28,6,512]{3,1,2,0:T(8,128)(2,1)S(1)} %get-tuple-element.226), channel_id=1, source_target_pairs={{1,0},{2,1},{3,2},{4,3},{5,4},{6,5},{7,6},{8,7},{9,8},{10,9},{11,1... | collective-permute-start | bytes 1032200 | tf_op jit(solution)/shard_map/ppermute | solution.py:18
  235.4 1.9 copy-start.1
  235.4 1.9 copy-start.6
  237.9 7.5 %copy-start.4 = (bf16[4,3,16,512]{3,2,1,0:T(8,128)(2,1)S(1)}, bf16[4,3,16,512]{3,2,1,0:T(8,128)(2,1)}, u32[]{:S(2)}) copy-start(bf16[4,3,16,512]{3,2,1,0:T(8,128)(2,1)} %get-tuple-element.144) | copy-start | bytes 589828
  237.9 10.7 %collective-permute-start.6 = (bf16[2,6,12,512]{3,1,2,0:T(8,128)(2,1)S(1)}, bf16[2,6,12,512]{3,1,2,0:T(8,128)(2,1)S(1)}, u32[]{:S(2)}, u32[]{:S(2)}) collective-permute-start(bf16[2,6,12,512]{3,1,2,0:T(8,128)(2,1)S(1)} %get-tuple-element.229), channel_id=1, source_target_pairs={{0,32},{32,64},{64,96},{96,128},{128,160},{160,192},{192,224},{224... | collective-permute-start | bytes 442376 | tf_op jit(solution)/shard_map/ppermute | solution.py:17
  242.7 8.9 %collective-permute-start.7 = (bf16[2,6,12,512]{3,1,2,0:T(8,128)(2,1)S(1)}, bf16[2,6,12,512]{3,1,2,0:T(8,128)(2,1)S(1)}, u32[]{:S(2)}, u32[]{:S(2)}) collective-permute-start(bf16[2,6,12,512]{3,1,2,0:T(8,128)(2,1)S(1)} %get-tuple-element.230), channel_id=1, source_target_pairs={{32,0},{64,32},{96,64},{128,96},{160,128},{192,160},{224,192},{256... | collective-permute-start | bytes 442376 | tf_op jit(solution)/shard_map/ppermute | solution.py:18
Sparse Core Ops, SparseCore 0:
  245.5 278.9 all-reduce.7
where the time goes:
time: 536 us; the launch traced here: 533 us
  waiting for transfers between devices  304 us (57%)
  local copies, waits for them, and re-layouts  137 us (26%)
  other arithmetic  35.6 us (7%)
  starting transfers between devices  23.2 us (4%)
  matrix products  15.5 us (3%)
  between operations  14.3 us (3%)
    psum x1, waiting for transfers between devices, shards(): total_weight = lax.psum(partial_weight, ('lat', 'lon'))  272 us
    dynamic_update_slice x8, local copies, waits for them, and re-layouts, strip_step(): lax.dynamic_update_slice_in_dim(grad_region, current + strip_grad, first_...  36.7 us
    ppermute x4, waiting for transfers between devices, extended(): after = lax.ppermute(initial, axis, down)  24.4 us
    slice x12, local copies, waits for them, and re-layouts, strip_step(): both[t]  24.1 us
    squeeze x12, local copies, waits for them, and re-layouts, strip_step(): both[t]  18 us
    ppermute x4, starting transfers between devices, extended(): before = lax.ppermute(last, axis, up)  16.2 us
    add x4, other arithmetic, strip_step(): current + strip_grad  15.1 us
    another operation x24, local copies, waits for them, and re-layouts, strip_step(): jnp.stack([band_patch[:, :, t * tile_side:t * tile_side + patch_side] for...  13.5 us
  transfers between devices with their start and end apart: 9, of which 9 were waited for; matrix products, arithmetic and copies ran while one was open for 1% of the time, Pallas kernels for 0%

commit v1 on v0

v1 whole, which is shorter than its diff:
```python
import functools
import math

import jax
import jax.numpy as jnp
from jax import lax
from jax.experimental import pallas as pl
from jax.experimental.pallas import tpu as pltpu
from jax.sharding import PartitionSpec as P

HEADS = 8
RADIUS = 6
MESH = pl.DeviceIdType.MESH
VMEM = pl.BlockSpec(memory_space=pltpu.VMEM)
N_LAT, N_LON, N_Z = 16, 32, 8
NEAR = [(u, v) for u in (-1, 0, 1) for v in (-1, 0, 1) if (u, v) != (0, 0)]
TAKE = {-1: (0, 1), 0: (0, 2), 1: (1, 1)}
LAND = {-1: (3, 1), 0: (1, 2), 1: (0, 1)}
OWNED = {-1: (0, 1), 0: (1, 2), 1: (3, 1)}


def near_device(side):
    lat, lon = lax.axis_index("lat"), lax.axis_index("lon")
    return (
        lax.rem(lat + side[0] + N_LAT, N_LAT),
        lax.rem(lon + side[1] + N_LON, N_LON),
    )


def block(ref, rows, cols):
    return ref.at[:, pl.ds(*rows), pl.ds(*cols)]


def enter(devices):
    barrier = pltpu.get_barrier_semaphore()
    for device in devices:
        pl.semaphore_signal(barrier, inc=1, device_id=device, device_id_type=MESH)
    pl.semaphore_wait(barrier, len(devices))


def halo_kernel(kv_ref, ext_ref, send_sems, recv_sems, own_sem):
    own = pltpu.make_async_copy(kv_ref, block(ext_ref, (1, 2), (1, 2)), own_sem)
    own.start()
    enter([near_device(side) for side in NEAR])
    copies = []
    for n, side in enumerate(NEAR):
        copy = pltpu.make_async_remote_copy(
            src_ref=block(kv_ref, TAKE[side[0]], TAKE[side[1]]),
            dst_ref=block(ext_ref, LAND[side[0]], LAND[side[1]]),
            send_sem=send_sems.at[n],
            recv_sem=recv_sems.at[n],
            device_id=near_device(side),
            device_id_type=MESH,
        )
        copy.start()
        copies.append(copy)
    own.wait()
    for copy in copies:
        copy.wait()


def dot_nt(a, b):
    return lax.dot_general(a, b, (((1,), (1,)), ((), ())), preferred_element_type=jnp.float32)


def attend_kernel(bias_ref, q_ref, k_ref, v_ref, w_ref, d_ref, dq_ref, dk_ref, dv_ref, pw_ref):
    upstream = d_ref[...]
    cells, width = q_ref.shape
    head = width // 2
    scale = head ** (-0.5)
    first = lax.broadcasted_iota(jnp.int32, (cells, width), 1) < head

    def pair(x):
        wide = x.astype(jnp.float32)
        both = jnp.concatenate([jnp.where(first, wide, 0.0), jnp.where(first, 0.0, wide)], axis=0)
        return both.astype(jnp.bfloat16)

    def unpair(x):
        return jnp.concatenate([x[:head, :cells], x[head:, cells:]], axis=0)

    mixed = pair(dot_nt(upstream, w_ref[...]).astype(jnp.bfloat16))
    query = pair(q_ref[...])
    key = k_ref[...]
    value = v_ref[...]
    scores = dot_nt(key, query) + bias_ref[...]
    peak = jnp.max(scores, axis=0, keepdims=True)
    lifted = jnp.exp2((scores - peak) * (scale * math.log2(math.e)))
    probs = lifted * (1.0 / jnp.sum(lifted, axis=0, keepdims=True))
    half = probs.astype(jnp.bfloat16)
    d_prob = dot_nt(value, mixed)
    delta = jnp.sum(half.astype(jnp.float32) * d_prob, axis=0, keepdims=True)
    d_score = (probs * (d_prob - delta)).astype(jnp.bfloat16)
    dk_ref[...] = (
        jnp.dot(d_score, query, preferred_element_type=jnp.float32) * scale
    ).astype(jnp.bfloat16)
    dv_ref[...] = jnp.dot(half, mixed, preferred_element_type=jnp.float32).astype(jnp.bfloat16)
    attended = unpair(jnp.dot(value.T, half, preferred_element_type=jnp.float32))
    pw_ref[...] = jnp.dot(
        attended.astype(jnp.bfloat16), upstream, preferred_element_type=jnp.float32
    ).astype(jnp.bfloat16)
    dq = unpair(jnp.dot(key.T, d_score, preferred_element_type=jnp.float32))
    dq_ref[...] = (dq.T * scale).astype(jnp.bfloat16)


def settle_kernel(
    weight_scale,
    grad_ref, part_ref,
    out_ref, weight_ref,
    side_a, side_b, corner, lat_in, q_out, q_in, z_in, gathered,
    near_send, near_recv, lat_send, lat_recv, q_send, q_recv, z_send, z_recv,
    f_send, f_recv, g_send, g_recv,
):
    lat, lon = lax.axis_index("lat"), lax.axis_index("lon")
    y_lo, z, core = lon // 16, lax.rem(lon // 2, 8), lax.rem(lon, 2)
    my_q = y_lo * 2 + core

    def lat_device(d):
        return (lax.rem(lat + d, N_LAT), lon)

    def q_of(d):
        return lax.rem(my_q + d, 4)

    def q_device(d):
        return (lat, (q_of(d) // 2) * 16 + z * 2 + lax.rem(q_of(d), 2))

    def z_device(d):
        return (lat, y_lo * 16 + lax.rem(z + d, N_Z) * 2 + core)

    def send(src, dst, send_sem, recv_sem, device):
        copy = pltpu.make_async_remote_copy(
            src_ref=src, dst_ref=dst, send_sem=send_sem, recv_sem=recv_sem,
            device_id=device, device_id_type=MESH,
        )
        copy.start()
        return copy

    enter(
        [near_device(side) for side in NEAR]
        + [lat_device(d) for d in range(1, N_LAT)]
        + [q_device(d) for d in range(1, 4)]
        + [z_device(d) for d in range(1, N_Z)]
    )
    sent = []
    lat_copies = [
        send(part_ref.at[lax.rem(lat + d, N_LAT)], lat_in.at[d], lat_send.at[d], lat_recv.at[d],
             lat_device(d))
        for d in range(1, N_LAT)
    ]
    near_copies, landed = [], []
    counts = [0, 0, 0]
    for n, side in enumerate(NEAR):
        kind = 2 if side[0] and side[1] else (0 if side[0] else 1)
        slot = (side_a, side_b, corner)[kind].at[counts[kind]]
        counts[kind] += 1
        near_copies.append(
            send(block(grad_ref, OWNED[side[0]], OWNED[side[1]]), slot, near_send.at[n],
                 near_recv.at[n], near_device(side))
        )
        landed.append((slot, TAKE[-side[0]], TAKE[-side[1]]))
    total = part_ref[lat].astype(jnp.float32)
    for d, copy in enumerate(lat_copies, 1):
        copy.wait_recv()
        total = total + lat_in[d].astype(jnp.float32)
    for j in range(4):
        q_out[j] = total[:, j * 128 : (j + 1) * 128]
    q_copies = [
        send(q_out.at[q_of(d)], q_in.at[d], q_send.at[d], q_recv.at[d], q_device(d))
        for d in range(1, 4)
    ]
    piece = q_out[my_q]
    for d, copy in enumerate(q_copies, 1):
        copy.wait_recv()
        piece = piece + q_in[d]
    z_in[z] = piece
    z_copies = [
        send(z_in.at[z], z_in.at[z], z_send.at[d], z_recv.at[d], z_device(d))
        for d in range(1, N_Z)
    ]
    for copy in near_copies:
        copy.wait_recv()
    for a in range(2):
        for b in range(2):
            owner = grad_ref[:, 1 + a, 1 + b].astype(jnp.float32)
            for slot, rows, cols in landed:
                i, j = a - rows[0], b - cols[0]
                if 0 <= i < rows[1] and 0 <= j < cols[1]:
                    owner = owner + slot[:, i, j].astype(jnp.float32)
            out_ref[:, a, b] = owner.astype(jnp.bfloat16)
    for copy in z_copies:
        copy.wait_recv()
    piece = z_in[0]
    for i in range(1, N_Z):
        piece = piece + z_in[i]
    gathered[my_q] = (piece * weight_scale).astype(jnp.bfloat16)
    f_copies = [
        send(gathered.at[my_q], gathered.at[my_q], f_send.at[d], f_recv.at[d], q_device(d))
        for d in range(1, 4)
    ]
    for copy in f_copies:
        copy.wait_recv()
    g_copies = [
        send(gathered, weight_ref.at[lat], g_send.at[d], g_recv.at[d], lat_device(d))
        for d in range(1, N_LAT)
    ]
    weight_ref[lat] = gathered[...]
    for copy in g_copies:
        copy.wait_recv()
    for copy in lat_copies + near_copies + q_copies + z_copies + f_copies + g_copies:
        copy.wait_send()


def to_quads(x):
    rows, cols, width = x.shape
    shaped = x.reshape(2, rows // 2, 2, cols // 2, width)
    return shaped.transpose(0, 2, 1, 3, 4).reshape(2, 2, rows * cols // 4, width)


def from_quads(x, rows, cols):
    width = x.shape[-1]
    shaped = x.reshape(2, 2, rows // 2, cols // 2, width)
    return shaped.transpose(0, 2, 1, 3, 4).reshape(rows, cols, width)


def window_bias(rows, cols, all_rows):
    high, wide = rows // 2, cols // 2

    def places(count):
        ids = jnp.arange(count * count * high * wide, dtype=jnp.int32)
        quad, cell = ids // (high * wide), ids % (high * wide)
        return (quad // count) * high + cell // wide, (quad % count) * wide + cell % wide

    key_row, key_col = places(4)
    key_row, key_col = key_row - high, key_col - wide
    row, col = places(2)
    grid_row = key_row + lax.axis_index("lat") * rows
    inside = (grid_row >= 0) & (grid_row < all_rows)
    near = (
        (jnp.abs(key_row[:, None] - row[None, :]) <= RADIUS)
        & (jnp.abs(key_col[:, None] - col[None, :]) <= RADIUS)
        & inside[:, None]
    )
    bias = jnp.where(near, 0.0, -1e30).astype(jnp.float32)
    return jnp.concatenate([bias, bias], axis=1)


def shards(queries, keys, values, out_weight, d_out):
    rows, cols, width = queries.shape
    all_rows = rows * N_LAT
    weight_scale = (all_rows * cols * N_LON) ** (-0.5)
    cells = rows * cols
    quad = cells // 4
    reach = 16 * quad
    bf16, f32 = jnp.bfloat16, jnp.float32
    dma = pltpu.SemaphoreType.DMA

    kv = jnp.stack([to_quads(keys), to_quads(values)])
    region = pl.pallas_call(
        halo_kernel,
        out_shape=jax.ShapeDtypeStruct((2, 4, 4, quad, width), bf16),
        in_specs=[VMEM],
        out_specs=VMEM,
        scratch_shapes=[dma((8,)), dma((8,)), dma],
        compiler_params=pltpu.CompilerParams(collective_id=0, has_side_effects=True),
        name="halo",
    )(kv)
    region = region.reshape(2, reach, width)
    query = to_quads(queries).reshape(cells, width)
    upstream = to_quads(d_out).reshape(cells, width)
    bias = window_bias(rows, cols, all_rows)
    pairs = HEADS // 2
    lanes = width // pairs
    part = pl.BlockSpec((cells, lanes), lambda h: (0, h))
    d_query, d_key, d_value, partial = pl.pallas_call(
        attend_kernel,
        grid=(pairs,),
        out_shape=(
            jax.ShapeDtypeStruct((cells, width), bf16),
            jax.ShapeDtypeStruct((reach, width), bf16),
            jax.ShapeDtypeStruct((reach, width), bf16),
            jax.ShapeDtypeStruct((width, width), bf16),
        ),
        in_specs=[
            pl.BlockSpec((reach, 2 * cells), lambda h: (0, 0)),
            part,
            pl.BlockSpec((None, reach, lanes), lambda h: (0, 0, h)),
            pl.BlockSpec((None, reach, lanes), lambda h: (1, 0, h)),
            pl.BlockSpec((lanes, width), lambda h: (h, 0)),
            pl.BlockSpec((cells, width), lambda h: (0, 0)),
        ],
        out_specs=(
            part,
            pl.BlockSpec((reach, lanes), lambda h: (0, h)),
            pl.BlockSpec((reach, lanes), lambda h: (0, h)),
            pl.BlockSpec((lanes, width), lambda h: (h, 0)),
        ),
        compiler_params=pltpu.CompilerParams(vmem_limit_bytes=48 << 20),
        name="attend",
    )(bias, query, region, region, out_weight, upstream)
    grads = jnp.stack([d_key, d_value]).reshape(2, 4, 4, quad, width)
    chunk = width // N_LAT
    settled, weight = pl.pallas_call(
        functools.partial(settle_kernel, weight_scale),
        out_shape=(
            jax.ShapeDtypeStruct((2, 2, 2, quad, width), bf16),
            jax.ShapeDtypeStruct((N_LAT, 4, chunk, width // 4), bf16),
        ),
        in_specs=[VMEM, VMEM],
        out_specs=(VMEM, VMEM),
        scratch_shapes=[
            pltpu.VMEM((2, 2, 1, 2, quad, width), bf16),
            pltpu.VMEM((2, 2, 2, 1, quad, width), bf16),
            pltpu.VMEM((4, 2, 1, 1, quad, width), bf16),
            pltpu.VMEM((N_LAT, chunk, width), bf16),
            pltpu.VMEM((4, chunk, width // 4), f32),
            pltpu.VMEM((4, chunk, width // 4), f32),
            pltpu.VMEM((N_Z, chunk, width // 4), f32),
            pltpu.VMEM((4, chunk, width // 4), bf16),
            dma((8,)), dma((8,)),
            dma((N_LAT,)), dma((N_LAT,)),
            dma((4,)), dma((4,)),
            dma((N_Z,)), dma((N_Z,)),
            dma((4,)), dma((4,)),
            dma((N_LAT,)), dma((N_LAT,)),
        ],
        compiler_params=pltpu.CompilerParams(
            collective_id=1, has_side_effects=True, vmem_limit_bytes=48 << 20
        ),
        name="settle",
    )(grads, partial.reshape(N_LAT, chunk, width))
    d_weight = weight.transpose(0, 2, 1, 3).reshape(width, width)
    return (
        from_quads(d_query.reshape(2, 2, quad, width), rows, cols),
        from_quads(settled[0], rows, cols),
        from_quads(settled[1], rows, cols),
        d_weight,
    )


def solution(mesh):
    placed = P("lat", "lon", None)
    return jax.shard_map(
        shards,
        mesh=mesh,
        in_specs=(placed, placed, placed, P(), placed),
        out_specs=(placed, placed, placed, P()),
        check_vma=False,
    )
```

time: 536 us -> 117 us (0.22)
  waiting for transfers between devices: 304 us -> 0 us
  local copies, waits for them, and re-layouts: 137 us -> 7.96 us
  Pallas kernels: 0 us -> 106 us
  other arithmetic: 35.6 us -> 1.72 us
  starting transfers between devices: 23.2 us -> 0 us
  matrix products: 15.5 us -> 0 us
  between operations: 14.3 us -> 0.8 us
    psum x1 -> x0, waiting for transfers between devices: 272 us -> none  [shards(): total_weight = lax.psum(partial_weight, ('lat', 'lon'))]
    pallas_call x0 -> x3, Pallas kernels: none -> 106 us  [the longest x1 61.9 us: shards(): pl.pallas_call(functools.partial(settle_kernel, weight_scale), out_shape=...]
    dynamic_update_slice x12 -> x0, local copies, waits for them, and re-layouts: 39.3 us -> none  [the longest x8 36.7 us: strip_step(): lax.dynamic_update_slice_in_dim(grad_region, current + strip_grad, first_...]
    ppermute x8 -> x0, waiting for transfers between devices: 32.5 us -> none  [the longest x4 24.4 us: extended(): after = lax.ppermute(initial, axis, down)]
    slice x19 -> x3, local copies, waits for them, and re-layouts: 32.5 us -> 0.44 us  [the longest x2 0.23 us: shards(): settled[1]]
    ppermute x8 -> x0, starting transfers between devices: 23.1 us -> none  [the longest x4 16.2 us: extended(): before = lax.ppermute(last, axis, up)]
    dynamic_slice x16 -> x0, local copies, waits for them, and re-layouts: 22.3 us -> none  [the longest x4 12.6 us: strip_step(): current = lax.dynamic_slice_in_dim(grad_region, first_row, patch_side, 1)]
    squeeze x12 -> x0, local copies, waits for them, and re-layouts: 18 us -> none  [strip_step(): both[t]]
  transfers between devices with their start and end apart: 9 -> 0, of which waited for: 9 -> 0; matrix products, arithmetic and copies ran while one was open for 1% -> 0% of each run, Pallas kernels for 0% -> 0%
where the time goes in v1:
time: 117 us; the launch traced here: 116 us
  Pallas kernels  106 us (91%)
  local copies, waits for them, and re-layouts  7.96 us (7%)
  other arithmetic  1.72 us (1%)
    pallas_call x1, Pallas kernels, shards(): pl.pallas_call(functools.partial(settle_kernel, weight_scale), out_shape=...  61.9 us
    pallas_call x1, Pallas kernels, shards(): pl.pallas_call(halo_kernel, out_shape=jax.ShapeDtypeStruct((2, 4, 4, quad...  35.2 us
    pallas_call x1, Pallas kernels, shards(): pl.pallas_call(attend_kernel, grid=(pairs,), out_shape=(jax.ShapeDtypeStr...  8.85 us
    reshape x4, local copies, waits for them, and re-layouts, to_quads(): shaped = x.reshape(2, rows // 2, 2, cols // 2, width)  2.54 us

profile of v1, /device:TPU:1, one launch (start us, length us, event | category | flops | bytes accessed | tf_op | source)
XLA Modules:
  0.0 116.4 jit_solution(7409390849924097297)
XLA Ops:
  0.6 0.0 copy-start.2
  0.7 0.0 copy-start.3
  0.7 1.2 %copy.26 = bf16[2,8,2,6,512]{4,2,3,1,0:T(2,128)(2,1)S(1)} copy(bf16[2,8,2,6,512]{4,1,0,3,2:T(8,128)(2,1)} %bitcast.54) | data formatting | bytes 393216 | tf_op jit(solution)/shard_map/reshape | solution.py:214
  1.9 1.1 copy.27
  3.1 0.8 pad_maximum_fusion.2.kv_ref
  3.9 0.0 copy-done.2
  3.9 0.1 copy.43
  4.0 0.1 reshape_reshape.9.q_ref
  4.1 0.0 copy-done.3
  4.1 0.1 copy.42
  4.2 0.1 reshape_reshape.10.d_ref
  4.3 0.5 fusion.2
  4.8 0.0 copy-start.1
  4.8 0.3 pad_maximum_fusion.1.bias_ref
  5.0 35.2 %halo.1 = bf16[2,4,4,48,512]{4,3,2,1,0:T(8,128)(2,1)} custom-call(bf16[2,2,2,48,512]{4,3,2,1,0:T(8,128)(2,1)} %pad_maximum_fusion.2.kv_ref), custom_call_target="tpu_custom_call" | custom-call | tf_op jit(solution)/shard_map/halo/pallas_call | solution.py:257
  40.2 0.0 copy-done.1
  40.2 0.0 copy-start
  40.2 1.4 %copy-done = bf16[2,4,4,48,512]{4,3,2,1,0:T(8,128)(2,1)S(1)} copy-done((bf16[2,4,4,48,512]{4,3,2,1,0:T(8,128)(2,1)S(1)}, bf16[2,4,4,48,512]{4,3,2,1,0:T(8,128)(2,1)}, u32[]{:S(2)}) %copy-start) | copy-done | bytes 1572888
  41.6 8.8 %attend.1 = (bf16[192,512]{1,0:T(8,128)(2,1)S(1)}, bf16[768,512]{1,0:T(8,128)(2,1)S(1)}, bf16[768,512]{1,0:T(8,128)(2,1)S(1)}, bf16[512,512]{1,0:T(8,128)(2,1)S(1)}) custom-call(f32[768,384]{1,0:T(8,128)S(1)} %pad_maximum_fusion.1.bias_ref, bf16[192,512]{1,0:T(8,128)(2,1)S(1)} %reshape_reshape.9.q_ref, bf16[2,768,512]{2,1,0:T(8,128)(2,1)S(1)} %bitcast.36, ...), custom_call_target="tpu_custom_call" | custom-call | tf_op jit(solution)/shard_map/attend/pallas_call | solution.py:273
  50.5 0.1 pad_maximum_fusion.grad_ref
  50.7 61.9 %settle.1 = (bf16[2,2,2,48,512]{4,3,2,1,0:T(8,128)(2,1)S(1)}, bf16[16,4,32,128]{3,2,1,0:T(8,128)(2,1)S(1)}) custom-call(bf16[2,4,4,48,512]{4,3,2,1,0:T(8,128)(2,1)S(1)} %pad_maximum_fusion.grad_ref, bf16[16,32,512]{2,1,0:T(8,128)(2,1)S(1)} %bitcast.41), custom_call_target="tpu_custom_call" | custom-call | tf_op jit(solution)/shard_map/settle/pallas_call | solution.py:301
  112.6 0.3 copy.36
  112.9 0.9 copy.41
  113.8 0.2 copy.34
  114.0 0.7 copy.35
  114.7 0.1 reshape_reshape.11
  114.8 0.7 copy.31
  115.5 0.2 copy.32
  115.7 0.7 copy.33
  (6 shorter events, 0.1 us)
Async XLA Ops:
  0.6 3.3 %copy-start.2 = (bf16[16,12,512]{2,0,1:T(8,128)(2,1)S(1)}, bf16[16,12,512]{2,0,1:T(8,128)(2,1)}, u32[]{:S(2)}) copy-start(bf16[16,12,512]{2,0,1:T(8,128)(2,1)} %param.5) | copy-start | bytes 589828
  0.7 3.4 %copy-start.3 = (bf16[16,12,512]{2,0,1:T(8,128)(2,1)S(1)}, bf16[16,12,512]{2,0,1:T(8,128)(2,1)}, u32[]{:S(2)}) copy-start(bf16[16,12,512]{2,0,1:T(8,128)(2,1)} %param.9) | copy-start | bytes 589828
  4.8 35.5 %copy-start.1 = (bf16[512,512]{1,0:T(8,128)(2,1)S(1)}, bf16[512,512]{1,0:T(8,128)(2,1)}, u32[]{:S(2)}) copy-start(bf16[512,512]{1,0:T(8,128)(2,1)} %w_ref.1) | copy-start | bytes 1572868
  40.2 1.4 %copy-start = (bf16[2,4,4,48,512]{4,3,2,1,0:T(8,128)(2,1)S(1)}, bf16[2,4,4,48,512]{4,3,2,1,0:T(8,128)(2,1)}, u32[]{:S(2)}) copy-start(bf16[2,4,4,48,512]{4,3,2,1,0:T(8,128)(2,1)} %halo.1) | copy-start | bytes 4718596

commit v2 on v1

v2 whole, which is shorter than its diff:
```python
import functools
import math

import jax
import jax.numpy as jnp
from jax import lax
from jax.experimental import pallas as pl
from jax.experimental.pallas import tpu as pltpu
from jax.sharding import PartitionSpec as P

HEADS = 8
RADIUS = 6
MESH = pl.DeviceIdType.MESH
VMEM = pl.BlockSpec(memory_space=pltpu.VMEM)
N_LAT, N_LON, N_Z, N_X, N_Y = 16, 32, 8, 4, 8
UP, DOWN, LEFT, RIGHT = (-1, 0), (1, 0), (0, -1), (0, 1)


def near_device(side):
    lat, lon = lax.axis_index("lat"), lax.axis_index("lon")
    return (
        lax.rem(lat + side[0] + N_LAT, N_LAT),
        lax.rem(lon + side[1] + N_LON, N_LON),
    )


def enter(devices):
    barrier = pltpu.get_barrier_semaphore()
    for device in devices:
        pl.semaphore_signal(barrier, inc=1, device_id=device, device_id_type=MESH)
    pl.semaphore_wait(barrier, len(devices))


class Sender:
    def __init__(self, send_sems, recv_sems):
        self.sems = (send_sems, recv_sems)
        self.copies = []

    def __call__(self, src, dst, device):
        n = len(self.copies)
        copy = pltpu.make_async_remote_copy(
            src_ref=src, dst_ref=dst, send_sem=self.sems[0].at[n], recv_sem=self.sems[1].at[n],
            device_id=device, device_id_type=MESH,
        )
        copy.start()
        self.copies.append(copy)
        return copy

    def finish(self):
        for copy in self.copies:
            copy.wait_send()


def halo_kernel(kv_ref, ext_ref, send_sems, recv_sems, own_sem):
    own = pltpu.make_async_copy(kv_ref, ext_ref.at[:, pl.ds(1, 2), pl.ds(1, 2)], own_sem)
    own.start()
    up, down, left, right = [near_device(side) for side in (UP, DOWN, LEFT, RIGHT)]
    enter([up, down, left, right])
    send = Sender(send_sems, recv_sems)
    middle = pl.ds(1, 2)
    rows = []
    for i in range(2):
        rows.append((i, 3, send(kv_ref.at[i, 0], ext_ref.at[i, 3, middle], up)))
        rows.append((i, 0, send(kv_ref.at[i, 1], ext_ref.at[i, 0, middle], down)))
    waits = [
        send(kv_ref.at[:, :, 0], ext_ref.at[:, middle, 3], left),
        send(kv_ref.at[:, :, 1], ext_ref.at[:, middle, 0], right),
    ]
    for i, row, copy in rows:
        copy.wait_recv()
        waits.append(send(ext_ref.at[i, row, 1], ext_ref.at[i, row, 3], left))
        waits.append(send(ext_ref.at[i, row, 2], ext_ref.at[i, row, 0], right))
    own.wait()
    for copy in waits:
        copy.wait_recv()
    send.finish()


def dot_nt(a, b):
    return lax.dot_general(a, b, (((1,), (1,)), ((), ())), preferred_element_type=jnp.float32)


def attend_kernel(bias_ref, q_ref, k_ref, v_ref, w_ref, d_ref, dq_ref, dk_ref, dv_ref, pw_ref):
    upstream = d_ref[...]
    cells, width = q_ref.shape
    head = width // 2
    scale = head ** (-0.5)
    first = lax.broadcasted_iota(jnp.int32, (cells, width), 1) < head

    def pair(x):
        wide = x.astype(jnp.float32)
        both = jnp.concatenate([jnp.where(first, wide, 0.0), jnp.where(first, 0.0, wide)], axis=0)
        return both.astype(jnp.bfloat16)

    def unpair(x):
        return jnp.concatenate([x[:head, :cells], x[head:, cells:]], axis=0)

    mixed = pair(dot_nt(upstream, w_ref[...]).astype(jnp.bfloat16))
    query = pair(q_ref[...])
    key = k_ref[...]
    value = v_ref[...]
    scores = dot_nt(key, query) + bias_ref[...]
    peak = jnp.max(scores, axis=0, keepdims=True)
    lifted = jnp.exp2((scores - peak) * (scale * math.log2(math.e)))
    probs = lifted * (1.0 / jnp.sum(lifted, axis=0, keepdims=True))
    half = probs.astype(jnp.bfloat16)
    d_prob = dot_nt(value, mixed)
    delta = jnp.sum(half.astype(jnp.float32) * d_prob, axis=0, keepdims=True)
    d_score = (probs * (d_prob - delta)).astype(jnp.bfloat16)
    dk_ref[...] = (
        jnp.dot(d_score, query, preferred_element_type=jnp.float32) * scale
    ).astype(jnp.bfloat16)
    dv_ref[...] = jnp.dot(half, mixed, preferred_element_type=jnp.float32).astype(jnp.bfloat16)
    attended = unpair(jnp.dot(value.T, half, preferred_element_type=jnp.float32))
    pw_ref[...] = jnp.dot(
        attended.astype(jnp.bfloat16), upstream, preferred_element_type=jnp.float32
    ).astype(jnp.bfloat16)
    dq = unpair(jnp.dot(key.T, d_score, preferred_element_type=jnp.float32))
    dq_ref[...] = (dq.T * scale).astype(jnp.bfloat16)


def settle_kernel(
    weight_scale,
    grad_ref, part_ref,
    out_ref, weight_ref,
    from_side, row_out, from_row,
    core_in, z_out, z_in, x_out, x_in, y_in, gathered,
    send_sems, recv_sems,
):
    f32, bf16 = jnp.float32, jnp.bfloat16
    lat, lon = lax.axis_index("lat"), lax.axis_index("lon")
    x, y_hi = lat // 4, lax.rem(lat, 4)
    y_lo, z, core = lon // 16, lax.rem(lon // 2, N_Z), lax.rem(lon, 2)
    my_y = y_hi * 2 + y_lo
    sibling = (lat, y_lo * 16 + z * 2 + 1 - core)
    up, down, left, right = [near_device(side) for side in (UP, DOWN, LEFT, RIGHT)]

    def z_device(d):
        return (lat, y_lo * 16 + lax.rem(z + d, N_Z) * 2 + core)

    def x_device(d):
        return (lax.rem(x + d, N_X) * 4 + y_hi, lon)

    def y_device(d):
        place = lax.rem(my_y + d, N_Y)
        return (x * 4 + place // 2, lax.rem(place, 2) * 16 + z * 2 + core)

    enter(
        [up, down, left, right, sibling]
        + [z_device(d) for d in range(1, N_Z)]
        + [x_device(d) for d in range(1, N_X)]
        + [y_device(d) for d in range(1, N_Y)]
    )
    send = Sender(send_sems, recv_sems)
    edges = []
    for row in (0, 3):
        edges.append(send(grad_ref.at[:, row, 0], from_side.at[1, :, row], left))
        edges.append(send(grad_ref.at[:, row, 3], from_side.at[0, :, row], right))
    order = [lax.rem(z + d, N_Z) for d in range(N_Z)]
    halves = {}
    for d in (4, 3, 5, 2, 6, 1, 7, 0):
        halves[d] = send(part_ref.at[1 - core, order[d]], core_in.at[order[d]], sibling)
    middle = pl.ds(1, 2)
    sides = [
        send(grad_ref.at[:, middle, 0], from_side.at[1, :, middle], left),
        send(grad_ref.at[:, middle, 3], from_side.at[0, :, middle], right),
    ]
    rows = []
    for n, (row, device) in enumerate(((0, up), (3, down))):
        for copy in edges[2 * n : 2 * n + 2]:
            copy.wait_recv()
        for b in range(2):
            row_out[n, :, b] = (
                grad_ref[:, row, 1 + b].astype(f32) + from_side[b, :, row].astype(f32)
            ).astype(bf16)
        rows.append(send(row_out.at[n], from_row.at[1 - n], device))
    z_copies = []
    total = None
    for d in (4, 3, 5, 2, 6, 1, 7, 0):
        halves[d].wait_recv()
        chip = part_ref[core, order[d]].astype(f32) + core_in[order[d]].astype(f32)
        if d:
            z_out[d] = chip.astype(bf16)
            z_copies.append((d, send(z_out.at[d], z_in.at[d], z_device(d))))
        else:
            total = chip
    for d, copy in z_copies:
        copy.wait_recv()
        total = total + z_in[d].astype(f32)
    lanes = x_out.shape[-1]
    for j in range(N_X):
        x_out[j] = total[:, j * lanes : (j + 1) * lanes]
    x_copies = [
        send(x_out.at[lax.rem(x + d, N_X)], x_in.at[d], x_device(d)) for d in range(1, N_X)
    ]
    piece = x_out[x]
    for d, copy in enumerate(x_copies, 1):
        copy.wait_recv()
        piece = piece + x_in[d]
    y_in[my_y] = piece
    y_copies = [send(y_in.at[my_y], y_in.at[my_y], y_device(d)) for d in range(1, N_Y)]
    for copy in sides + rows:
        copy.wait_recv()
    for a in range(2):
        for b in range(2):
            out_ref[:, a, b] = (
                grad_ref[:, 1 + a, 1 + b].astype(f32)
                + from_side[b, :, 1 + a].astype(f32)
                + from_row[a, :, b].astype(f32)
            ).astype(bf16)
    for copy in y_copies:
        copy.wait_recv()
    piece = y_in[0]
    for i in range(1, N_Y):
        piece = piece + y_in[i]
    gathered[x] = (piece * weight_scale).astype(bf16)
    x_copies = [send(gathered.at[x], gathered.at[x], x_device(d)) for d in range(1, N_X)]
    for copy in x_copies:
        copy.wait_recv()
    z_copies = [
        (d, send(gathered, weight_ref.at[core, z], z_device(d))) for d in (4, 3, 5, 2, 6, 1, 7)
    ]
    last = [send(gathered, weight_ref.at[core, z], sibling)]
    weight_ref[core, z] = gathered[...]
    for d, copy in reversed(z_copies):
        copy.wait_recv()
        block = weight_ref.at[core, lax.rem(z + N_Z - d, N_Z)]
        last.append(send(block, block, sibling))
    for copy in last:
        copy.wait_recv()
    send.finish()


def to_quads(x):
    rows, cols, width = x.shape
    shaped = x.reshape(2, rows // 2, 2, cols // 2, width)
    return shaped.transpose(0, 2, 1, 3, 4).reshape(2, 2, rows * cols // 4, width)


def from_quads(x, rows, cols):
    width = x.shape[-1]
    shaped = x.reshape(2, 2, rows // 2, cols // 2, width)
    return shaped.transpose(0, 2, 1, 3, 4).reshape(rows, cols, width)


def window_bias(rows, cols, all_rows):
    high, wide = rows // 2, cols // 2

    def places(count):
        ids = jnp.arange(count * count * high * wide, dtype=jnp.int32)
        quad, cell = ids // (high * wide), ids % (high * wide)
        return (quad // count) * high + cell // wide, (quad % count) * wide + cell % wide

    key_row, key_col = places(4)
    key_row, key_col = key_row - high, key_col - wide
    row, col = places(2)
    grid_row = key_row + lax.axis_index("lat") * rows
    inside = (grid_row >= 0) & (grid_row < all_rows)
    near = (
        (jnp.abs(key_row[:, None] - row[None, :]) <= RADIUS)
        & (jnp.abs(key_col[:, None] - col[None, :]) <= RADIUS)
        & inside[:, None]
    )
    bias = jnp.where(near, 0.0, -1e30).astype(jnp.float32)
    return jnp.concatenate([bias, bias], axis=1)


def shards(queries, keys, values, out_weight, d_out):
    rows, cols, width = queries.shape
    all_rows = rows * N_LAT
    weight_scale = (all_rows * cols * N_LON) ** (-0.5)
    cells = rows * cols
    quad = cells // 4
    reach = 16 * quad
    bf16, f32 = jnp.bfloat16, jnp.float32
    dma = pltpu.SemaphoreType.DMA

    kv = jnp.stack([to_quads(keys), to_quads(values)])
    region = pl.pallas_call(
        halo_kernel,
        out_shape=jax.ShapeDtypeStruct((2, 4, 4, quad, width), bf16),
        in_specs=[VMEM],
        out_specs=VMEM,
        scratch_shapes=[dma((14,)), dma((14,)), dma],
        compiler_params=pltpu.CompilerParams(collective_id=0, has_side_effects=True),
        name="halo",
    )(kv)
    region = region.reshape(2, reach, width)
    query = to_quads(queries).reshape(cells, width)
    upstream = to_quads(d_out).reshape(cells, width)
    bias = window_bias(rows, cols, all_rows)
    pairs = HEADS // 2
    lanes = width // pairs
    part = pl.BlockSpec((cells, lanes), lambda h: (0, h))
    d_query, d_key, d_value, partial = pl.pallas_call(
        attend_kernel,
        grid=(pairs,),
        out_shape=(
            jax.ShapeDtypeStruct((cells, width), bf16),
            jax.ShapeDtypeStruct((reach, width), bf16),
            jax.ShapeDtypeStruct((reach, width), bf16),
            jax.ShapeDtypeStruct((width, width), bf16),
        ),
        in_specs=[
            pl.BlockSpec((reach, 2 * cells), lambda h: (0, 0)),
            part,
            pl.BlockSpec((None, reach, lanes), lambda h: (0, 0, h)),
            pl.BlockSpec((None, reach, lanes), lambda h: (1, 0, h)),
            pl.BlockSpec((lanes, width), lambda h: (h, 0)),
            pl.BlockSpec((cells, width), lambda h: (0, 0)),
        ],
        out_specs=(
            part,
            pl.BlockSpec((reach, lanes), lambda h: (0, h)),
            pl.BlockSpec((reach, lanes), lambda h: (0, h)),
            pl.BlockSpec((lanes, width), lambda h: (h, 0)),
        ),
        compiler_params=pltpu.CompilerParams(vmem_limit_bytes=48 << 20),
        name="attend",
    )(bias, query, region, region, out_weight, upstream)
    grads = jnp.stack([d_key, d_value]).reshape(2, 4, 4, quad, width)
    chunk = width // (2 * N_Z)
    settled, weight = pl.pallas_call(
        functools.partial(settle_kernel, weight_scale),
        out_shape=(
            jax.ShapeDtypeStruct((2, 2, 2, quad, width), bf16),
            jax.ShapeDtypeStruct((2, N_Z, N_X, chunk, lanes), bf16),
        ),
        in_specs=[VMEM, VMEM],
        out_specs=(VMEM, VMEM),
        scratch_shapes=[
            pltpu.VMEM((2, 2, 4, quad, width), bf16),
            pltpu.VMEM((2, 2, 2, quad, width), bf16),
            pltpu.VMEM((2, 2, 2, quad, width), bf16),
            pltpu.VMEM((N_Z, chunk, width), bf16),
            pltpu.VMEM((N_Z, chunk, width), bf16),
            pltpu.VMEM((N_Z, chunk, width), bf16),
            pltpu.VMEM((N_X, chunk, lanes), f32),
            pltpu.VMEM((N_X, chunk, lanes), f32),
            pltpu.VMEM((N_Y, chunk, lanes), f32),
            pltpu.VMEM((N_X, chunk, lanes), bf16),
            dma((51,)), dma((51,)),
        ],
        compiler_params=pltpu.CompilerParams(
            collective_id=1, has_side_effects=True, vmem_limit_bytes=48 << 20
        ),
        name="settle",
    )(grads, partial.reshape(2, N_Z, chunk, width))
    d_weight = weight.transpose(0, 1, 3, 2, 4).reshape(width, width)
    return (
        from_quads(d_query.reshape(2, 2, quad, width), rows, cols),
        from_quads(settled[0], rows, cols),
        from_quads(settled[1], rows, cols),
        d_weight,
    )


def solution(mesh):
    placed = P("lat", "lon", None)
    return jax.shard_map(
        shards,
        mesh=mesh,
        in_specs=(placed, placed, placed, P(), placed),
        out_specs=(placed, placed, placed, P()),
        check_vma=False,
    )
```

time: 117 us -> 90.9 us (0.78)
  Pallas kernels: 106 us -> 80.2 us
    pallas_call x1, Pallas kernels: 61.9 us -> 44.3 us  [shards(): pl.pallas_call(functools.partial(settle_kernel, weight_scale), out_shape=...]
    pallas_call x1, Pallas kernels: 35.2 us -> 27 us  [shards(): pl.pallas_call(halo_kernel, out_shape=jax.ShapeDtypeStruct((2, 4, 4, quad...]
where the time goes in v2:
time: 90.9 us; the launch traced here: 90.7 us
  Pallas kernels  80.2 us (88%)
  local copies, waits for them, and re-layouts  7.96 us (9%)
  other arithmetic  1.72 us (2%)
    pallas_call x1, Pallas kernels, shards(): pl.pallas_call(functools.partial(settle_kernel, weight_scale), out_shape=...  44.3 us
    pallas_call x1, Pallas kernels, shards(): pl.pallas_call(halo_kernel, out_shape=jax.ShapeDtypeStruct((2, 4, 4, quad...  27 us
    pallas_call x1, Pallas kernels, shards(): pl.pallas_call(attend_kernel, grid=(pairs,), out_shape=(jax.ShapeDtypeStr...  8.84 us
    reshape x4, local copies, waits for them, and re-layouts, to_quads(): shaped = x.reshape(2, rows // 2, 2, cols // 2, width)  2.54 us
    unnamed x9, local copies, waits for them, and re-layouts  2.29 us
    transpose x3, local copies, waits for them, and re-layouts, from_quads(): return shaped.transpose(0, 2, 1, 3, 4).reshape(rows, cols, width)  2.17 us

profile of v2, /device:TPU:1, one launch (start us, length us, event | category | flops | bytes accessed | tf_op | source)
XLA Modules:
  0.0 90.7 jit_solution(4355612844635256019)
XLA Ops:
  0.6 0.0 copy-start.2
  0.7 0.0 copy-start.3
  0.7 1.2 %copy.26 = bf16[2,8,2,6,512]{4,2,3,1,0:T(2,128)(2,1)S(1)} copy(bf16[2,8,2,6,512]{4,1,0,3,2:T(8,128)(2,1)} %bitcast.54) | data formatting | bytes 393216 | tf_op jit(solution)/shard_map/reshape | solution.py:236
  1.9 1.1 %copy.27 = bf16[2,8,2,6,512]{4,2,3,1,0:T(2,128)(2,1)S(1)} copy(bf16[2,8,2,6,512]{4,1,0,3,2:T(8,128)(2,1)} %bitcast.55) | data formatting | bytes 393216 | tf_op jit(solution)/shard_map/reshape | solution.py:236
  3.1 0.8 pad_maximum_fusion.2.kv_ref
  3.9 0.0 copy-done.2
  3.9 0.1 copy.43
  4.0 0.1 reshape_reshape.9.q_ref
  4.1 0.0 copy-done.3
  4.1 0.1 copy.42
  4.2 0.1 reshape_reshape.10.d_ref
  4.3 0.5 fusion.2
  4.8 0.0 copy-start.1
  4.8 0.3 pad_maximum_fusion.1.bias_ref
  5.0 27.0 %halo.1 = bf16[2,4,4,48,512]{4,3,2,1,0:T(8,128)(2,1)} custom-call(bf16[2,2,2,48,512]{4,3,2,1,0:T(8,128)(2,1)} %pad_maximum_fusion.2.kv_ref), custom_call_target="tpu_custom_call" | custom-call | tf_op jit(solution)/shard_map/halo/pallas_call | solution.py:279
  32.0 0.0 copy-done.1
  32.1 0.0 copy-start
  32.1 1.4 %copy-done = bf16[2,4,4,48,512]{4,3,2,1,0:T(8,128)(2,1)S(1)} copy-done((bf16[2,4,4,48,512]{4,3,2,1,0:T(8,128)(2,1)S(1)}, bf16[2,4,4,48,512]{4,3,2,1,0:T(8,128)(2,1)}, u32[]{:S(2)}) %copy-start) | copy-done | bytes 1572888
  33.5 8.8 %attend.1 = (bf16[192,512]{1,0:T(8,128)(2,1)S(1)}, bf16[768,512]{1,0:T(8,128)(2,1)S(1)}, bf16[768,512]{1,0:T(8,128)(2,1)S(1)}, bf16[512,512]{1,0:T(8,128)(2,1)S(1)}) custom-call(f32[768,384]{1,0:T(8,128)S(1)} %pad_maximum_fusion.1.bias_ref, bf16[192,512]{1,0:T(8,128)(2,1)S(1)} %reshape_reshape.9.q_ref, bf16[2,768,512]{2,1,0:T(8,128)(2,1)S(1)} %bitcast.36, ...), custom_call_target="tpu_custom_call" | custom-call | tf_op jit(solution)/shard_map/attend/pallas_call | solution.py:295
  42.3 0.1 pad_maximum_fusion.grad_ref
  42.5 44.3 %settle.1 = (bf16[2,2,2,48,512]{4,3,2,1,0:T(8,128)(2,1)S(1)}, bf16[2,8,4,32,128]{4,3,2,1,0:T(8,128)(2,1)S(1)}) custom-call(bf16[2,4,4,48,512]{4,3,2,1,0:T(8,128)(2,1)S(1)} %pad_maximum_fusion.grad_ref, bf16[2,8,32,512]{3,2,1,0:T(8,128)(2,1)S(1)} %bitcast.41), custom_call_target="tpu_custom_call" | custom-call | tf_op jit(solution)/shard_map/settle/pallas_call | solution.py:323
  86.8 0.3 copy.36
  87.1 0.9 copy.41
  88.0 0.2 copy.34
  88.2 0.7 copy.35
  88.9 0.1 reshape_reshape.11
  89.0 0.7 copy.31
  89.7 0.2 copy.32
  89.9 0.7 copy.33
  (6 shorter events, 0.1 us)
Async XLA Ops:
  0.6 3.3 %copy-start.2 = (bf16[16,12,512]{2,0,1:T(8,128)(2,1)S(1)}, bf16[16,12,512]{2,0,1:T(8,128)(2,1)}, u32[]{:S(2)}) copy-start(bf16[16,12,512]{2,0,1:T(8,128)(2,1)} %param.5) | copy-start | bytes 589828
  0.7 3.4 %copy-start.3 = (bf16[16,12,512]{2,0,1:T(8,128)(2,1)S(1)}, bf16[16,12,512]{2,0,1:T(8,128)(2,1)}, u32[]{:S(2)}) copy-start(bf16[16,12,512]{2,0,1:T(8,128)(2,1)} %param.9) | copy-start | bytes 589828
  4.8 27.3 %copy-start.1 = (bf16[512,512]{1,0:T(8,128)(2,1)S(1)}, bf16[512,512]{1,0:T(8,128)(2,1)}, u32[]{:S(2)}) copy-start(bf16[512,512]{1,0:T(8,128)(2,1)} %w_ref.1) | copy-start | bytes 1572868
  32.1 1.4 %copy-start = (bf16[2,4,4,48,512]{4,3,2,1,0:T(8,128)(2,1)S(1)}, bf16[2,4,4,48,512]{4,3,2,1,0:T(8,128)(2,1)}, u32[]{:S(2)}) copy-start(bf16[2,4,4,48,512]{4,3,2,1,0:T(8,128)(2,1)} %halo.1) | copy-start | bytes 4718596

commit v3 on v2

--- a/solution.py
+++ b/solution.py
@@ -124,7 +124,7 @@
     grad_ref, part_ref,
     out_ref, weight_ref,
     from_side, row_out, from_row,
-    core_in, z_out, z_in, x_out, x_in, y_in, gathered,
+    core_in, x_out, x_in, z_out, z_in, y_in, gathered,
     send_sems, recv_sems,
 ):
     f32, bf16 = jnp.float32, jnp.bfloat16
@@ -156,10 +156,20 @@
     for row in (0, 3):
         edges.append(send(grad_ref.at[:, row, 0], from_side.at[1, :, row], left))
         edges.append(send(grad_ref.at[:, row, 3], from_side.at[0, :, row], right))
-    order = [lax.rem(z + d, N_Z) for d in range(N_Z)]
+    order = [lax.rem(x + d, N_X) for d in range(N_X)]
     halves = {}
-    for d in (4, 3, 5, 2, 6, 1, 7, 0):
+    for d in (2, 1, 3, 0):
         halves[d] = send(part_ref.at[1 - core, order[d]], core_in.at[order[d]], sibling)
+    x_copies = []
+    total = None
+    for d in (2, 1, 3, 0):
+        halves[d].wait_recv()
+        chip = part_ref[core, order[d]].astype(f32) + core_in[order[d]].astype(f32)
+        if d:
+            x_out[d] = chip.astype(bf16)
+            x_copies.append((d, send(x_out.at[d], x_in.at[d], x_device(d))))
+        else:
+            total = chip
     middle = pl.ds(1, 2)
     sides = [
         send(grad_ref.at[:, middle, 0], from_side.at[1, :, middle], left),
@@ -174,31 +184,36 @@
                 grad_ref[:, row, 1 + b].astype(f32) + from_side[b, :, row].astype(f32)
             ).astype(bf16)
         rows.append(send(row_out.at[n], from_row.at[1 - n], device))
-    z_copies = []
-    total = None
-    for d in (4, 3, 5, 2, 6, 1, 7, 0):
-        halves[d].wait_recv()
-        chip = part_ref[core, order[d]].astype(f32) + core_in[order[d]].astype(f32)
-        if d:
-            z_out[d] = chip.astype(bf16)
-            z_copies.append((d, send(z_out.at[d], z_in.at[d], z_device(d))))
-        else:
-            total = chip
+    for d, copy in x_copies:
+        copy.wait_recv()
+        total = total + x_in[d].astype(f32)
+    high, lanes = z_out.shape[1:]
+    across = total.shape[1] // lanes
+    for n in range(N_Z):
+        i, j = n // across, n % across
+        z_out[n] = total[i * high : (i + 1) * high, j * lanes : (j + 1) * lanes].astype(bf16)
+    far_first = (4, 3, 5, 2, 6, 1, 7)
+    z_copies = [
+        (d, send(z_out.at[lax.rem(z + d, N_Z)], z_in.at[d], z_device(d))) for d in far_first
+    ]
+    piece = z_out[z].astype(f32)
     for d, copy in z_copies:
         copy.wait_recv()
-        total = total + z_in[d].astype(f32)
-    lanes = x_out.shape[-1]
-    for j in range(N_X):
-        x_out[j] = total[:, j * lanes : (j + 1) * lanes]
-    x_copies = [
-        send(x_out.at[lax.rem(x + d, N_X)], x_in.at[d], x_device(d)) for d in range(1, N_X)
-    ]
-    piece = x_out[x]
-    for d, copy in enumerate(x_copies, 1):
-        copy.wait_recv()
-        piece = piece + x_in[d]
-    y_in[my_y] = piece
-    y_copies = [send(y_in.at[my_y], y_in.at[my_y], y_device(d)) for d in range(1, N_Y)]
+        piece = piece + z_in[d].astype(f32)
+    y_in[my_y] = piece.astype(bf16)
+    y_copies = [send(y_in.at[my_y], y_in.at[my_y], y_device(d)) for d in far_first]
+    for copy in y_copies:
+        copy.wait_recv()
+    piece = y_in[0].astype(f32)
+    for i in range(1, N_Y):
+        piece = piece + y_in[i].astype(f32)
+    gathered[z] = (piece * weight_scale).astype(bf16)
+    z_copies = [send(gathered.at[z], gathered.at[z], z_device(d)) for d in far_first]
+    for copy in z_copies:
+        copy.wait_recv()
+    x_copies = [(d, send(gathered, weight_ref.at[core, x], x_device(d))) for d in (2, 1, 3)]
+    last = [send(gathered, weight_ref.at[core, x], sibling)]
+    weight_ref[core, x] = gathered[...]
     for copy in sides + rows:
         copy.wait_recv()
     for a in range(2):
@@ -208,23 +223,9 @@
                 + from_side[b, :, 1 + a].astype(f32)
                 + from_row[a, :, b].astype(f32)
             ).astype(bf16)
-    for copy in y_copies:
-        copy.wait_recv()
-    piece = y_in[0]
-    for i in range(1, N_Y):
-        piece = piece + y_in[i]
-    gathered[x] = (piece * weight_scale).astype(bf16)
-    x_copies = [send(gathered.at[x], gathered.at[x], x_device(d)) for d in range(1, N_X)]
-    for copy in x_copies:
-        copy.wait_recv()
-    z_copies = [
-        (d, send(gathered, weight_ref.at[core, z], z_device(d))) for d in (4, 3, 5, 2, 6, 1, 7)
-    ]
-    last = [send(gathered, weight_ref.at[core, z], sibling)]
-    weight_ref[core, z] = gathered[...]
-    for d, copy in reversed(z_copies):
-        copy.wait_recv()
-        block = weight_ref.at[core, lax.rem(z + N_Z - d, N_Z)]
+    for d, copy in reversed(x_copies):
+        copy.wait_recv()
+        block = weight_ref.at[core, lax.rem(x + N_X - d, N_X)]
         last.append(send(block, block, sibling))
     for copy in last:
         copy.wait_recv()
@@ -319,12 +320,13 @@
         name="attend",
     )(bias, query, region, region, out_weight, upstream)
     grads = jnp.stack([d_key, d_value]).reshape(2, 4, 4, quad, width)
-    chunk = width // (2 * N_Z)
+    chunk = width // (2 * N_X)
+    high = chunk * pairs // N_Z
     settled, weight = pl.pallas_call(
         functools.partial(settle_kernel, weight_scale),
         out_shape=(
             jax.ShapeDtypeStruct((2, 2, 2, quad, width), bf16),
-            jax.ShapeDtypeStruct((2, N_Z, N_X, chunk, lanes), bf16),
+            jax.ShapeDtypeStruct((2, N_X, N_Z, high, lanes), bf16),
         ),
         in_specs=[VMEM, VMEM],
         out_specs=(VMEM, VMEM),
@@ -332,21 +334,21 @@
             pltpu.VMEM((2, 2, 4, quad, width), bf16),
             pltpu.VMEM((2, 2, 2, quad, width), bf16),
             pltpu.VMEM((2, 2, 2, quad, width), bf16),
-            pltpu.VMEM((N_Z, chunk, width), bf16),
-            pltpu.VMEM((N_Z, chunk, width), bf16),
-            pltpu.VMEM((N_Z, chunk, width), bf16),
-            pltpu.VMEM((N_X, chunk, lanes), f32),
-            pltpu.VMEM((N_X, chunk, lanes), f32),
-            pltpu.VMEM((N_Y, chunk, lanes), f32),
-            pltpu.VMEM((N_X, chunk, lanes), bf16),
-            dma((51,)), dma((51,)),
+            pltpu.VMEM((N_X, chunk, width), bf16),
+            pltpu.VMEM((N_X, chunk, width), bf16),
+            pltpu.VMEM((N_X, chunk, width), bf16),
+            pltpu.VMEM((N_Z, high, lanes), bf16),
+            pltpu.VMEM((N_Z, high, lanes), bf16),
+            pltpu.VMEM((N_Y, high, lanes), bf16),
+            pltpu.VMEM((N_Z, high, lanes), bf16),
+            dma((43,)), dma((43,)),
         ],
         compiler_params=pltpu.CompilerParams(
             collective_id=1, has_side_effects=True, vmem_limit_bytes=48 << 20
         ),
         name="settle",
-    )(grads, partial.reshape(2, N_Z, chunk, width))
-    d_weight = weight.transpose(0, 1, 3, 2, 4).reshape(width, width)
+    )(grads, partial.reshape(2, N_X, chunk, width))
+    d_weight = weight.reshape(-1, pairs, high, lanes).transpose(0, 2, 1, 3).reshape(width, width)
     return (
         from_quads(d_query.reshape(2, 2, quad, width), rows, cols),
         from_quads(settled[0], rows, cols),

time: 90.9 us -> 85.3 us (0.938)
  Pallas kernels: 80.2 us -> 74.5 us
    pallas_call x1, Pallas kernels: 44.3 us -> 38.7 us  [shards(): pl.pallas_call(functools.partial(settle_kernel, weight_scale), out_shape=...]
where the time goes in v3:
time: 85.3 us; the launch traced here: 85 us
  Pallas kernels  74.5 us (87%)
  local copies, waits for them, and re-layouts  7.96 us (9%)
  other arithmetic  1.72 us (2%)
    pallas_call x1, Pallas kernels, shards(): pl.pallas_call(functools.partial(settle_kernel, weight_scale), out_shape=...  38.7 us
    pallas_call x1, Pallas kernels, shards(): pl.pallas_call(halo_kernel, out_shape=jax.ShapeDtypeStruct((2, 4, 4, quad...  27 us
    pallas_call x1, Pallas kernels, shards(): pl.pallas_call(attend_kernel, grid=(pairs,), out_shape=(jax.ShapeDtypeStr...  8.84 us
    reshape x4, local copies, waits for them, and re-layouts, to_quads(): shaped = x.reshape(2, rows // 2, 2, cols // 2, width)  2.54 us
    unnamed x9, local copies, waits for them, and re-layouts  2.29 us
    transpose x3, local copies, waits for them, and re-layouts, from_quads(): return shaped.transpose(0, 2, 1, 3, 4).reshape(rows, cols, width)  2.17 us

profile of v3, /device:TPU:1, one launch (start us, length us, event | category | flops | bytes accessed | tf_op | source)
XLA Modules:
  0.0 85.0 jit_solution(3759488131939019758)
XLA Ops:
  0.6 0.0 copy-start.2
  0.7 0.0 copy-start.3
  0.7 1.2 %copy.27 = bf16[2,8,2,6,512]{4,2,3,1,0:T(2,128)(2,1)S(1)} copy(bf16[2,8,2,6,512]{4,1,0,3,2:T(8,128)(2,1)} %bitcast.56) | data formatting | bytes 393216 | tf_op jit(solution)/shard_map/reshape | solution.py:237
  1.9 1.1 %copy.28 = bf16[2,8,2,6,512]{4,2,3,1,0:T(2,128)(2,1)S(1)} copy(bf16[2,8,2,6,512]{4,1,0,3,2:T(8,128)(2,1)} %bitcast.57) | data formatting | bytes 393216 | tf_op jit(solution)/shard_map/reshape | solution.py:237
  3.1 0.8 pad_maximum_fusion.2.kv_ref
  3.9 0.0 copy-done.2
  3.9 0.1 copy.44
  4.0 0.1 reshape_reshape.9.q_ref
  4.1 0.0 copy-done.3
  4.1 0.1 copy.43
  4.2 0.1 reshape_reshape.10.d_ref
  4.3 0.5 fusion.2
  4.8 0.0 copy-start.1
  4.8 0.3 pad_maximum_fusion.1.bias_ref
  5.0 27.0 %halo.1 = bf16[2,4,4,48,512]{4,3,2,1,0:T(8,128)(2,1)} custom-call(bf16[2,2,2,48,512]{4,3,2,1,0:T(8,128)(2,1)} %pad_maximum_fusion.2.kv_ref), custom_call_target="tpu_custom_call" | custom-call | tf_op jit(solution)/shard_map/halo/pallas_call | solution.py:280
  32.0 0.0 copy-done.1
  32.1 0.0 copy-start
  32.1 1.4 %copy-done = bf16[2,4,4,48,512]{4,3,2,1,0:T(8,128)(2,1)S(1)} copy-done((bf16[2,4,4,48,512]{4,3,2,1,0:T(8,128)(2,1)S(1)}, bf16[2,4,4,48,512]{4,3,2,1,0:T(8,128)(2,1)}, u32[]{:S(2)}) %copy-start) | copy-done | bytes 1572888
  33.5 8.8 %attend.1 = (bf16[192,512]{1,0:T(8,128)(2,1)S(1)}, bf16[768,512]{1,0:T(8,128)(2,1)S(1)}, bf16[768,512]{1,0:T(8,128)(2,1)S(1)}, bf16[512,512]{1,0:T(8,128)(2,1)S(1)}) custom-call(f32[768,384]{1,0:T(8,128)S(1)} %pad_maximum_fusion.1.bias_ref, bf16[192,512]{1,0:T(8,128)(2,1)S(1)} %reshape_reshape.9.q_ref, bf16[2,768,512]{2,1,0:T(8,128)(2,1)S(1)} %bitcast.38, ...), custom_call_target="tpu_custom_call" | custom-call | tf_op jit(solution)/shard_map/attend/pallas_call | solution.py:296
  42.3 0.1 pad_maximum_fusion.grad_ref
  42.5 38.7 %settle.1 = (bf16[2,2,2,48,512]{4,3,2,1,0:T(8,128)(2,1)S(1)}, bf16[2,4,8,32,128]{4,3,2,1,0:T(8,128)(2,1)S(1)}) custom-call(bf16[2,4,4,48,512]{4,3,2,1,0:T(8,128)(2,1)S(1)} %pad_maximum_fusion.grad_ref, bf16[2,4,64,512]{3,2,1,0:T(8,128)(2,1)S(1)} %bitcast.43), custom_call_target="tpu_custom_call" | custom-call | tf_op jit(solution)/shard_map/settle/pallas_call | solution.py:325
  81.2 0.3 copy.37
  81.5 0.9 %copy.42 = bf16[64,8,4,128]{3,1,2,0:T(8,128)(2,1)} copy(bf16[64,8,4,128]{3,2,1,0:T(4,128)(2,1)S(1)} %bitcast.44) | data formatting | bytes 1048576
  82.4 0.2 copy.35
  82.6 0.7 copy.36
  83.3 0.1 reshape_reshape.11
  83.4 0.7 copy.32
  84.1 0.2 copy.33
  84.3 0.7 copy.34
  (6 shorter events, 0.1 us)
Async XLA Ops:
  0.6 3.3 %copy-start.2 = (bf16[16,12,512]{2,0,1:T(8,128)(2,1)S(1)}, bf16[16,12,512]{2,0,1:T(8,128)(2,1)}, u32[]{:S(2)}) copy-start(bf16[16,12,512]{2,0,1:T(8,128)(2,1)} %param.5) | copy-start | bytes 589828
  0.7 3.4 %copy-start.3 = (bf16[16,12,512]{2,0,1:T(8,128)(2,1)S(1)}, bf16[16,12,512]{2,0,1:T(8,128)(2,1)}, u32[]{:S(2)}) copy-start(bf16[16,12,512]{2,0,1:T(8,128)(2,1)} %param.9) | copy-start | bytes 589828
  4.8 27.3 %copy-start.1 = (bf16[512,512]{1,0:T(8,128)(2,1)S(1)}, bf16[512,512]{1,0:T(8,128)(2,1)}, u32[]{:S(2)}) copy-start(bf16[512,512]{1,0:T(8,128)(2,1)} %w_ref.1) | copy-start | bytes 1572868
  32.1 1.4 %copy-start = (bf16[2,4,4,48,512]{4,3,2,1,0:T(8,128)(2,1)S(1)}, bf16[2,4,4,48,512]{4,3,2,1,0:T(8,128)(2,1)}, u32[]{:S(2)}) copy-start(bf16[2,4,4,48,512]{4,3,2,1,0:T(8,128)(2,1)} %halo.1) | copy-start | bytes 4718596

commit v4 on v3

v4 whole, which is shorter than its diff:
```python
import functools
import math

import jax
import jax.numpy as jnp
from jax import lax
from jax.experimental import pallas as pl
from jax.experimental.pallas import tpu as pltpu
from jax.sharding import PartitionSpec as P

HEADS = 8
RADIUS = 6
MESH = pl.DeviceIdType.MESH
VMEM = pl.BlockSpec(memory_space=pltpu.VMEM)
N_LAT, N_LON, N_Z, N_X, N_Y = 16, 32, 8, 4, 8
UP, DOWN, LEFT, RIGHT = (-1, 0), (1, 0), (0, -1), (0, 1)


def near_device(side):
    lat, lon = lax.axis_index("lat"), lax.axis_index("lon")
    return (
        lax.rem(lat + side[0] + N_LAT, N_LAT),
        lax.rem(lon + side[1] + N_LON, N_LON),
    )


def enter(devices):
    barrier = pltpu.get_barrier_semaphore()
    for device in devices:
        pl.semaphore_signal(barrier, inc=1, device_id=device, device_id_type=MESH)
    pl.semaphore_wait(barrier, len(devices))


class Sender:
    def __init__(self, send_sems, recv_sems):
        self.sems = (send_sems, recv_sems)
        self.copies = []

    def __call__(self, src, dst, device):
        n = len(self.copies)
        copy = pltpu.make_async_remote_copy(
            src_ref=src, dst_ref=dst, send_sem=self.sems[0].at[n], recv_sem=self.sems[1].at[n],
            device_id=device, device_id_type=MESH,
        )
        copy.start()
        self.copies.append(copy)
        return copy

    def finish(self):
        for copy in self.copies:
            copy.wait_send()


def dot_nt(a, b):
    return lax.dot_general(a, b, (((1,), (1,)), ((), ())), preferred_element_type=jnp.float32)


def whole_kernel(
    weight_scale,
    bias_ref, q_ref, kv_ref, w_ref, d_ref,
    dq_ref, out_ref, weight_ref,
    ext_ref, grad_ref, part_ref, query_ref, mixed_ref, probs_ref, half_ref,
    from_side, row_out, from_row,
    core_in, x_out, x_in, z_out, z_in, y_in, gathered,
    send_sems, recv_sems, own_sem,
):
    f32, bf16 = jnp.float32, jnp.bfloat16
    lat, lon = lax.axis_index("lat"), lax.axis_index("lon")
    x, y_hi = lat // 4, lax.rem(lat, 4)
    y_lo, z, core = lon // 16, lax.rem(lon // 2, N_Z), lax.rem(lon, 2)
    my_y = y_hi * 2 + y_lo
    sibling = (lat, y_lo * 16 + z * 2 + 1 - core)
    up, down, left, right = [near_device(side) for side in (UP, DOWN, LEFT, RIGHT)]

    def z_device(d):
        return (lat, y_lo * 16 + lax.rem(z + d, N_Z) * 2 + core)

    def x_device(d):
        return (lax.rem(x + d, N_X) * 4 + y_hi, lon)

    def y_device(d):
        place = lax.rem(my_y + d, N_Y)
        return (x * 4 + place // 2, lax.rem(place, 2) * 16 + z * 2 + core)

    enter(
        [up, down, left, right, sibling]
        + [z_device(d) for d in range(1, N_Z)]
        + [x_device(d) for d in range(1, N_X)]
        + [y_device(d) for d in range(1, N_Y)]
    )
    send = Sender(send_sems, recv_sems)
    middle = pl.ds(1, 2)
    own = pltpu.make_async_copy(kv_ref, ext_ref.at[:, middle, middle], own_sem)
    own.start()
    arrivals = []
    for i in range(2):
        arrivals.append((i, 3, send(kv_ref.at[i, 0], ext_ref.at[i, 3, middle], up)))
        arrivals.append((i, 0, send(kv_ref.at[i, 1], ext_ref.at[i, 0, middle], down)))
    waits = [
        send(kv_ref.at[:, :, 0], ext_ref.at[:, middle, 3], left),
        send(kv_ref.at[:, :, 1], ext_ref.at[:, middle, 0], right),
    ]
    cells, width = q_ref.shape
    pairs = HEADS // 2
    wide = width // pairs
    head = wide // 2
    scale = head ** (-0.5)
    first = lax.broadcasted_iota(jnp.int32, (cells, wide), 1) < head

    def lanes_of(h):
        return slice(h * wide, (h + 1) * wide)

    def pair(value):
        value = value.astype(f32)
        both = jnp.concatenate([jnp.where(first, value, 0.0), jnp.where(first, 0.0, value)], axis=0)
        return both.astype(bf16)

    def unpair(value):
        return jnp.concatenate([value[:head, :cells], value[head:, cells:]], axis=0)

    def reached(i, h):
        return ext_ref[i, :, :, :, lanes_of(h)].reshape(-1, wide)

    for h in range(pairs):
        query_ref[h] = pair(q_ref[:, lanes_of(h)])
        mixed_ref[h] = pair(dot_nt(d_ref[...], w_ref[lanes_of(h), :]).astype(bf16))
    for i, row, copy in arrivals:
        copy.wait_recv()
        waits.append(send(ext_ref.at[i, row, 1], ext_ref.at[i, row, 3], left))
        waits.append(send(ext_ref.at[i, row, 2], ext_ref.at[i, row, 0], right))
    own.wait()
    for copy in waits:
        copy.wait_recv()

    def forward(h):
        scores = dot_nt(reached(0, h), query_ref[h]) + bias_ref[...]
        peak = jnp.max(scores, axis=0, keepdims=True)
        lifted = jnp.exp2((scores - peak) * (scale * math.log2(math.e)))
        probs = lifted * (1.0 / jnp.sum(lifted, axis=0, keepdims=True))
        half = probs.astype(bf16)
        probs_ref[h] = probs
        half_ref[h] = half
        attended = unpair(jnp.dot(reached(1, h).T, half, preferred_element_type=f32))
        part = jnp.dot(attended.astype(bf16), d_ref[...], preferred_element_type=f32)
        chunk = part_ref.shape[2]
        for n in range(wide // chunk):
            at = h * (wide // chunk) + n
            part_ref[at // N_X, at % N_X] = part[n * chunk : (n + 1) * chunk].astype(bf16)

    def backward(h):
        half, mixed = half_ref[h], mixed_ref[h]
        key = reached(0, h)
        d_prob = dot_nt(reached(1, h), mixed)
        delta = jnp.sum(half.astype(f32) * d_prob, axis=0, keepdims=True)
        d_score = (probs_ref[h] * (d_prob - delta)).astype(bf16)
        d_key = jnp.dot(d_score, query_ref[h], preferred_element_type=f32) * scale
        d_value = jnp.dot(half, mixed, preferred_element_type=f32)
        for i, grad in enumerate((d_key, d_value)):
            grad_ref[i, :, :, :, lanes_of(h)] = grad.astype(bf16).reshape(4, 4, -1, wide)
        dq = unpair(jnp.dot(key.T, d_score, preferred_element_type=f32))
        dq_ref[:, lanes_of(h)] = (dq.T * scale).astype(bf16)

    for h in range(pairs):
        forward(h)
    backward(0)
    order = [lax.rem(x + d, N_X) for d in range(N_X)]
    halves = {}
    for d in (2, 1, 3, 0):
        halves[d] = send(part_ref.at[1 - core, order[d]], core_in.at[order[d]], sibling)
    backward(1)
    x_copies = []
    total = None
    for d in (2, 1, 3, 0):
        halves[d].wait_recv()
        chip = part_ref[core, order[d]].astype(f32) + core_in[order[d]].astype(f32)
        if d:
            x_out[d] = chip.astype(bf16)
            x_copies.append((d, send(x_out.at[d], x_in.at[d], x_device(d))))
        else:
            total = chip
    backward(2)
    backward(3)
    for d, copy in x_copies:
        copy.wait_recv()
        total = total + x_in[d].astype(f32)
    high, lanes = z_out.shape[1:]
    across = total.shape[1] // lanes
    for n in range(N_Z):
        i, j = n // across, n % across
        z_out[n] = total[i * high : (i + 1) * high, j * lanes : (j + 1) * lanes].astype(bf16)
    far_first = (4, 3, 5, 2, 6, 1, 7)
    z_copies = [
        (d, send(z_out.at[lax.rem(z + d, N_Z)], z_in.at[d], z_device(d))) for d in far_first
    ]
    edges = []
    for row in (0, 3):
        edges.append(send(grad_ref.at[:, row, 0], from_side.at[1, :, row], left))
        edges.append(send(grad_ref.at[:, row, 3], from_side.at[0, :, row], right))
    sides = [
        send(grad_ref.at[:, middle, 0], from_side.at[1, :, middle], left),
        send(grad_ref.at[:, middle, 3], from_side.at[0, :, middle], right),
    ]
    piece = z_out[z].astype(f32)
    for d, copy in z_copies:
        copy.wait_recv()
        piece = piece + z_in[d].astype(f32)
    y_in[my_y] = piece.astype(bf16)
    y_copies = [send(y_in.at[my_y], y_in.at[my_y], y_device(d)) for d in far_first]
    rows = []
    for n, (row, device) in enumerate(((0, up), (3, down))):
        for copy in edges[2 * n : 2 * n + 2]:
            copy.wait_recv()
        for b in range(2):
            row_out[n, :, b] = (
                grad_ref[:, row, 1 + b].astype(f32) + from_side[b, :, row].astype(f32)
            ).astype(bf16)
        rows.append(send(row_out.at[n], from_row.at[1 - n], device))
    for copy in y_copies:
        copy.wait_recv()
    piece = y_in[0].astype(f32)
    for i in range(1, N_Y):
        piece = piece + y_in[i].astype(f32)
    gathered[z] = (piece * weight_scale).astype(bf16)
    z_copies = [send(gathered.at[z], gathered.at[z], z_device(d)) for d in far_first]
    for copy in z_copies:
        copy.wait_recv()
    x_copies = [(d, send(gathered, weight_ref.at[core, x], x_device(d))) for d in (2, 1, 3)]
    last = [send(gathered, weight_ref.at[core, x], sibling)]
    weight_ref[core, x] = gathered[...]
    for copy in sides + rows:
        copy.wait_recv()
    for a in range(2):
        for b in range(2):
            out_ref[:, a, b] = (
                grad_ref[:, 1 + a, 1 + b].astype(f32)
                + from_side[b, :, 1 + a].astype(f32)
                + from_row[a, :, b].astype(f32)
            ).astype(bf16)
    for d, copy in reversed(x_copies):
        copy.wait_recv()
        block = weight_ref.at[core, lax.rem(x + N_X - d, N_X)]
        last.append(send(block, block, sibling))
    for copy in last:
        copy.wait_recv()
    send.finish()


def to_quads(x):
    rows, cols, width = x.shape
    shaped = x.reshape(2, rows // 2, 2, cols // 2, width)
    return shaped.transpose(0, 2, 1, 3, 4).reshape(2, 2, rows * cols // 4, width)


def from_quads(x, rows, cols):
    width = x.shape[-1]
    shaped = x.reshape(2, 2, rows // 2, cols // 2, width)
    return shaped.transpose(0, 2, 1, 3, 4).reshape(rows, cols, width)


def window_bias(rows, cols, all_rows):
    high, wide = rows // 2, cols // 2

    def places(count):
        ids = jnp.arange(count * count * high * wide, dtype=jnp.int32)
        quad, cell = ids // (high * wide), ids % (high * wide)
        return (quad // count) * high + cell // wide, (quad % count) * wide + cell % wide

    key_row, key_col = places(4)
    key_row, key_col = key_row - high, key_col - wide
    row, col = places(2)
    grid_row = key_row + lax.axis_index("lat") * rows
    inside = (grid_row >= 0) & (grid_row < all_rows)
    near = (
        (jnp.abs(key_row[:, None] - row[None, :]) <= RADIUS)
        & (jnp.abs(key_col[:, None] - col[None, :]) <= RADIUS)
        & inside[:, None]
    )
    bias = jnp.where(near, 0.0, -1e30).astype(jnp.float32)
    return jnp.concatenate([bias, bias], axis=1)


def shards(queries, keys, values, out_weight, d_out):
    rows, cols, width = queries.shape
    all_rows = rows * N_LAT
    weight_scale = (all_rows * cols * N_LON) ** (-0.5)
    cells = rows * cols
    quad = cells // 4
    reach = 16 * quad
    bf16, f32 = jnp.bfloat16, jnp.float32
    dma = pltpu.SemaphoreType.DMA

    kv = jnp.stack([to_quads(keys), to_quads(values)])
    query = to_quads(queries).reshape(cells, width)
    upstream = to_quads(d_out).reshape(cells, width)
    bias = window_bias(rows, cols, all_rows)
    pairs = HEADS // 2
    lanes = width // pairs
    chunk = width // (2 * N_X)
    high = chunk * pairs // N_Z
    d_query, settled, weight = pl.pallas_call(
        functools.partial(whole_kernel, weight_scale),
        out_shape=(
            jax.ShapeDtypeStruct((cells, width), bf16),
            jax.ShapeDtypeStruct((2, 2, 2, quad, width), bf16),
            jax.ShapeDtypeStruct((2, N_X, N_Z, high, lanes), bf16),
        ),
        in_specs=[VMEM] * 5,
        out_specs=(VMEM, VMEM, VMEM),
        scratch_shapes=[
            pltpu.VMEM((2, 4, 4, quad, width), bf16),
            pltpu.VMEM((2, 4, 4, quad, width), bf16),
            pltpu.VMEM((2, N_X, chunk, width), bf16),
            pltpu.VMEM((pairs, 2 * cells, lanes), bf16),
            pltpu.VMEM((pairs, 2 * cells, lanes), bf16),
            pltpu.VMEM((pairs, reach, 2 * cells), f32),
            pltpu.VMEM((pairs, reach, 2 * cells), bf16),
            pltpu.VMEM((2, 2, 4, quad, width), bf16),
            pltpu.VMEM((2, 2, 2, quad, width), bf16),
            pltpu.VMEM((2, 2, 2, quad, width), bf16),
            pltpu.VMEM((N_X, chunk, width), bf16),
            pltpu.VMEM((N_X, chunk, width), bf16),
            pltpu.VMEM((N_X, chunk, width), bf16),
            pltpu.VMEM((N_Z, high, lanes), bf16),
            pltpu.VMEM((N_Z, high, lanes), bf16),
            pltpu.VMEM((N_Y, high, lanes), bf16),
            pltpu.VMEM((N_Z, high, lanes), bf16),
            dma((57,)), dma((57,)), dma,
        ],
        compiler_params=pltpu.CompilerParams(
            collective_id=0, has_side_effects=True, vmem_limit_bytes=48 << 20
        ),
        name="whole",
    )(bias, query, kv, out_weight, upstream)
    d_weight = weight.reshape(-1, pairs, high, lanes).transpose(0, 2, 1, 3).reshape(width, width)
    return (
        from_quads(d_query.reshape(2, 2, quad, width), rows, cols),
        from_quads(settled[0], rows, cols),
        from_quads(settled[1], rows, cols),
        d_weight,
    )


def solution(mesh):
    placed = P("lat", "lon", None)
    return jax.shard_map(
        shards,
        mesh=mesh,
        in_specs=(placed, placed, placed, P(), placed),
        out_specs=(placed, placed, placed, P()),
        check_vma=False,
    )
```

time: 85.3 us -> 75 us (0.88)
  Pallas kernels: 74.5 us -> 65.9 us
  other arithmetic: 1.72 us -> 0.83 us
    pallas_call x3 -> x1, Pallas kernels: 74.5 us -> 65.9 us  [shards(): pl.pallas_call(functools.partial(whole_kernel, weight_scale), out_shape=(...]
    unnamed x9 -> x7, local copies, waits for them, and re-layouts: 2.29 us -> 1.65 us
where the time goes in v4:
time: 75 us; the launch traced here: 74.8 us
  Pallas kernels  65.9 us (88%)
  local copies, waits for them, and re-layouts  7.37 us (10%)
  other arithmetic  0.83 us (1%)
  between operations  0.78 us (1%)
    pallas_call x1, Pallas kernels, shards(): pl.pallas_call(functools.partial(whole_kernel, weight_scale), out_shape=(...  65.9 us
    reshape x4, local copies, waits for them, and re-layouts, to_quads(): shaped = x.reshape(2, rows // 2, 2, cols // 2, width)  2.57 us
    transpose x3, local copies, waits for them, and re-layouts, from_quads(): return shaped.transpose(0, 2, 1, 3, 4).reshape(rows, cols, width)  2.17 us
    unnamed x7, local copies, waits for them, and re-layouts  1.65 us

profile of v4, /device:TPU:1, one launch (start us, length us, event | category | flops | bytes accessed | tf_op | source)
XLA Modules:
  0.0 74.8 jit_solution(2689548895853572468)
XLA Ops:
  0.7 0.0 copy-start.1
  0.7 1.2 %copy.27 = bf16[2,8,2,6,512]{4,2,3,1,0:T(2,128)(2,1)S(1)} copy(bf16[2,8,2,6,512]{4,1,0,3,2:T(8,128)(2,1)} %bitcast.47) | data formatting | bytes 393216 | tf_op jit(solution)/shard_map/reshape | solution.py:250
  1.9 0.0 copy-start.2
  1.9 1.2 %copy.28 = bf16[2,8,2,6,512]{4,2,3,1,0:T(2,128)(2,1)S(1)} copy(bf16[2,8,2,6,512]{4,1,0,3,2:T(8,128)(2,1)} %bitcast.48) | data formatting | bytes 393216 | tf_op jit(solution)/shard_map/reshape | solution.py:250
  3.2 0.0 copy-done.1
  3.2 0.1 copy.44
  3.3 0.1 reshape_reshape.9.q_ref
  3.4 0.0 copy-done.2
  3.4 0.1 copy.43
  3.5 0.1 reshape_reshape.10.d_ref
  3.6 0.5 fusion.2
  4.1 0.0 copy-start
  4.1 0.3 pad_maximum_fusion.bias_ref
  4.4 0.8 %copy-done = bf16[512,512]{1,0:T(8,128)(2,1)S(1)} copy-done((bf16[512,512]{1,0:T(8,128)(2,1)S(1)}, bf16[512,512]{1,0:T(8,128)(2,1)}, u32[]{:S(2)}) %copy-start) | copy-done | bytes 524312
  5.1 65.9 %whole.1 = (bf16[192,512]{1,0:T(8,128)(2,1)S(1)}, bf16[2,2,2,48,512]{4,3,2,1,0:T(8,128)(2,1)S(1)}, bf16[2,4,8,32,128]{4,3,2,1,0:T(8,128)(2,1)S(1)}) custom-call(f32[768,384]{1,0:T(8,128)S(1)} %pad_maximum_fusion.bias_ref, bf16[192,512]{1,0:T(8,128)(2,1)S(1)} %reshape_reshape.9.q_ref, bf16[2,2,2,48,512]{4,3,2,1,0:T(8,128)(2,1)S(1)} %pad_maximum_fusion.1.kv_ref, ...), custom_call_target="tpu_custom_call" | custom-call | tf_op jit(solution)/shard_map/whole/pallas_call | solution.py:300
  71.0 0.1 reshape_reshape.11
  71.1 0.7 copy.32
  71.8 0.2 copy.35
  72.0 0.7 copy.36
  72.8 0.2 copy.33
  73.0 0.7 copy.34
  73.7 0.3 copy.37
  74.0 0.9 %copy.42 = bf16[64,8,4,128]{3,1,2,0:T(8,128)(2,1)} copy(bf16[64,8,4,128]{3,2,1,0:T(4,128)(2,1)S(1)} %bitcast.35) | data formatting | bytes 1048576
  (7 shorter events, 0.2 us)
Async XLA Ops:
  0.7 2.5 %copy-start.1 = (bf16[16,12,512]{2,0,1:T(8,128)(2,1)S(1)}, bf16[16,12,512]{2,0,1:T(8,128)(2,1)}, u32[]{:S(2)}) copy-start(bf16[16,12,512]{2,0,1:T(8,128)(2,1)} %param.5) | copy-start | bytes 589828
  1.9 1.5 %copy-start.2 = (bf16[16,12,512]{2,0,1:T(8,128)(2,1)S(1)}, bf16[16,12,512]{2,0,1:T(8,128)(2,1)}, u32[]{:S(2)}) copy-start(bf16[16,12,512]{2,0,1:T(8,128)(2,1)} %param.9) | copy-start | bytes 589828
  4.1 1.0 %copy-start = (bf16[512,512]{1,0:T(8,128)(2,1)S(1)}, bf16[512,512]{1,0:T(8,128)(2,1)}, u32[]{:S(2)}) copy-start(bf16[512,512]{1,0:T(8,128)(2,1)} %w_ref.1) | copy-start | bytes 1572868

commit v5 on v4

--- a/solution.py
+++ b/solution.py
@@ -55,11 +55,29 @@
     return lax.dot_general(a, b, (((1,), (1,)), ((), ())), preferred_element_type=jnp.float32)
 
 
+def quad_of(ref, a, b):
+    rows, cols, _ = ref.shape
+    high, wide = rows // 2, cols // 2
+    strips = [
+        ref[a * high + i].astype(jnp.float32)[b * wide : (b + 1) * wide] for i in range(high)
+    ]
+    return jnp.concatenate(strips, axis=0).astype(jnp.bfloat16)
+
+
+def put_rows(ref, a, west, east, lanes):
+    rows, cols, _ = ref.shape
+    high, wide = rows // 2, cols // 2
+    for i in range(high):
+        cut = slice(i * wide, (i + 1) * wide)
+        row = jnp.concatenate([west[cut], east[cut]], axis=0)
+        ref[a * high + i, :, lanes] = row.astype(jnp.bfloat16)
+
+
 def whole_kernel(
     weight_scale,
-    bias_ref, q_ref, kv_ref, w_ref, d_ref,
-    dq_ref, out_ref, weight_ref,
-    ext_ref, grad_ref, part_ref, query_ref, mixed_ref, probs_ref, half_ref,
+    bias_ref, queries_ref, keys_ref, values_ref, w_ref, d_out_ref,
+    dq_ref, dk_ref, dv_ref, full_ref,
+    weight_ref, q_ref, d_ref, kv_ref, ext_ref, grad_ref, part_ref, query_ref, mixed_ref, probs_ref, half_ref,
     from_side, row_out, from_row,
     core_in, x_out, x_in, z_out, z_in, y_in, gathered,
     send_sems, recv_sems, own_sem,
@@ -82,6 +100,10 @@
         place = lax.rem(my_y + d, N_Y)
         return (x * 4 + place // 2, lax.rem(place, 2) * 16 + z * 2 + core)
 
+    for i, field in enumerate((keys_ref, values_ref)):
+        for a in range(2):
+            for b in range(2):
+                kv_ref[i, a, b] = quad_of(field, a, b)
     enter(
         [up, down, left, right, sibling]
         + [z_device(d) for d in range(1, N_Z)]
@@ -121,6 +143,11 @@
     def reached(i, h):
         return ext_ref[i, :, :, :, lanes_of(h)].reshape(-1, wide)
 
+    for a in range(2):
+        for b in range(2):
+            at = (2 * a + b) * (cells // 4)
+            q_ref[at : at + cells // 4] = quad_of(queries_ref, a, b)
+            d_ref[at : at + cells // 4] = quad_of(d_out_ref, a, b)
     for h in range(pairs):
         query_ref[h] = pair(q_ref[:, lanes_of(h)])
         mixed_ref[h] = pair(dot_nt(d_ref[...], w_ref[lanes_of(h), :]).astype(bf16))
@@ -158,7 +185,11 @@
         for i, grad in enumerate((d_key, d_value)):
             grad_ref[i, :, :, :, lanes_of(h)] = grad.astype(bf16).reshape(4, 4, -1, wide)
         dq = unpair(jnp.dot(key.T, d_score, preferred_element_type=f32))
-        dq_ref[:, lanes_of(h)] = (dq.T * scale).astype(bf16)
+        dq = dq.T * scale
+        size = cells // 4
+        for a in range(2):
+            at = 2 * a * size
+            put_rows(dq_ref, a, dq[at : at + size], dq[at + size : at + 2 * size], lanes_of(h))
 
     for h in range(pairs):
         forward(h)
@@ -229,32 +260,27 @@
     weight_ref[core, x] = gathered[...]
     for copy in sides + rows:
         copy.wait_recv()
-    for a in range(2):
-        for b in range(2):
-            out_ref[:, a, b] = (
-                grad_ref[:, 1 + a, 1 + b].astype(f32)
-                + from_side[b, :, 1 + a].astype(f32)
-                + from_row[a, :, b].astype(f32)
-            ).astype(bf16)
+    for i, result in enumerate((dk_ref, dv_ref)):
+        for a in range(2):
+            sums = [
+                grad_ref[i, 1 + a, 1 + b].astype(f32)
+                + from_side[b, i, 1 + a].astype(f32)
+                + from_row[a, i, b].astype(f32)
+                for b in range(2)
+            ]
+            put_rows(result, a, sums[0], sums[1], slice(None))
     for d, copy in reversed(x_copies):
         copy.wait_recv()
         block = weight_ref.at[core, lax.rem(x + N_X - d, N_X)]
         last.append(send(block, block, sibling))
     for copy in last:
         copy.wait_recv()
+    for at in range(2 * N_X * N_Z):
+        c, k, n = at // (N_X * N_Z), at // N_Z % N_X, at % N_Z
+        row = (c * N_X + k) * N_Z // across * high + n // across * high
+        col = n % across * lanes
+        full_ref[row : row + high, col : col + lanes] = weight_ref[c, k, n]
     send.finish()
-
-
-def to_quads(x):
-    rows, cols, width = x.shape
-    shaped = x.reshape(2, rows // 2, 2, cols // 2, width)
-    return shaped.transpose(0, 2, 1, 3, 4).reshape(2, 2, rows * cols // 4, width)
-
-
-def from_quads(x, rows, cols):
-    width = x.shape[-1]
-    shaped = x.reshape(2, 2, rows // 2, cols // 2, width)
-    return shaped.transpose(0, 2, 1, 3, 4).reshape(rows, cols, width)
 
 
 def window_bias(rows, cols, all_rows):
@@ -289,24 +315,22 @@
     bf16, f32 = jnp.bfloat16, jnp.float32
     dma = pltpu.SemaphoreType.DMA
 
-    kv = jnp.stack([to_quads(keys), to_quads(values)])
-    query = to_quads(queries).reshape(cells, width)
-    upstream = to_quads(d_out).reshape(cells, width)
     bias = window_bias(rows, cols, all_rows)
     pairs = HEADS // 2
     lanes = width // pairs
     chunk = width // (2 * N_X)
     high = chunk * pairs // N_Z
-    d_query, settled, weight = pl.pallas_call(
+    field = jax.ShapeDtypeStruct((rows, cols, width), bf16)
+    return pl.pallas_call(
         functools.partial(whole_kernel, weight_scale),
-        out_shape=(
-            jax.ShapeDtypeStruct((cells, width), bf16),
-            jax.ShapeDtypeStruct((2, 2, 2, quad, width), bf16),
-            jax.ShapeDtypeStruct((2, N_X, N_Z, high, lanes), bf16),
-        ),
-        in_specs=[VMEM] * 5,
-        out_specs=(VMEM, VMEM, VMEM),
+        out_shape=(field, field, field, jax.ShapeDtypeStruct((width, width), bf16)),
+        in_specs=[VMEM] * 6,
+        out_specs=(VMEM,) * 4,
         scratch_shapes=[
+            pltpu.VMEM((2, N_X, N_Z, high, lanes), bf16),
+            pltpu.VMEM((cells, width), bf16),
+            pltpu.VMEM((cells, width), bf16),
+            pltpu.VMEM((2, 2, 2, quad, width), bf16),
             pltpu.VMEM((2, 4, 4, quad, width), bf16),
             pltpu.VMEM((2, 4, 4, quad, width), bf16),
             pltpu.VMEM((2, N_X, chunk, width), bf16),
@@ -330,14 +354,7 @@
             collective_id=0, has_side_effects=True, vmem_limit_bytes=48 << 20
         ),
         name="whole",
-    )(bias, query, kv, out_weight, upstream)
-    d_weight = weight.reshape(-1, pairs, high, lanes).transpose(0, 2, 1, 3).reshape(width, width)
-    return (
-        from_quads(d_query.reshape(2, 2, quad, width), rows, cols),
-        from_quads(settled[0], rows, cols),
-        from_quads(settled[1], rows, cols),
-        d_weight,
-    )
+    )(bias, queries, keys, values, out_weight, d_out)
 
 
 def solution(mesh):

time: 75 us -> 74.9 us (level)
    unnamed x7 -> x9, local copies, waits for them, and re-layouts: 1.65 us -> 4.81 us
    reshape x4 -> x0, local copies, waits for them, and re-layouts: 2.57 us -> none  [to_quads(): shaped = x.reshape(2, rows // 2, 2, cols // 2, width)]
    transpose x4 -> x0, local copies, waits for them, and re-layouts: 2.44 us -> none  [the longest x3 2.17 us: from_quads(): return shaped.transpose(0, 2, 1, 3, 4).reshape(rows, cols, width)]
    pallas_call x0 -> x3, local copies, waits for them, and re-layouts: none -> 2.37 us  [shards(): pl.pallas_call(functools.partial(whole_kernel, weight_scale), out_shape=(...]
where the time goes in v5:
time: 74.9 us; the launch traced here: 74.6 us
  Pallas kernels  66 us (88%)
  local copies, waits for them, and re-layouts  7.18 us (10%)
  other arithmetic  0.79 us (1%)
    pallas_call x1, Pallas kernels, shards(): pl.pallas_call(functools.partial(whole_kernel, weight_scale), out_shape=(...  66 us
    unnamed x9, local copies, waits for them, and re-layouts  4.81 us
    pallas_call x3, local copies, waits for them, and re-layouts, shards(): pl.pallas_call(functools.partial(whole_kernel, weight_scale), out_shape=(...  2.37 us

profile of v5, /device:TPU:1, one launch (start us, length us, event | category | flops | bytes accessed | tf_op | source)
XLA Modules:
  0.0 74.6 jit_solution(17323049177579351468)
XLA Ops:
  0.6 0.0 copy-start.1
  0.7 1.0 %copy.9.queries_ref = bf16[16,12,512]{2,1,0:T(8,128)(2,1)S(1)} copy(bf16[16,12,512]{2,0,1:T(8,128)(2,1)} %param.5) | data formatting | bytes 393216 | tf_op args[0]
  1.8 1.0 %copy.10.keys_ref = bf16[16,12,512]{2,1,0:T(8,128)(2,1)S(1)} copy(bf16[16,12,512]{2,0,1:T(8,128)(2,1)} %param.6) | data formatting | bytes 393216 | tf_op args[1]
  2.8 1.0 %copy.11.values_ref = bf16[16,12,512]{2,1,0:T(8,128)(2,1)S(1)} copy(bf16[16,12,512]{2,0,1:T(8,128)(2,1)} %param.7) | data formatting | bytes 393216 | tf_op args[2]
  3.9 0.0 copy-done.1
  3.9 0.1 copy.12.d_out_ref
  4.0 0.5 fusion.2
  4.5 0.0 copy-start
  4.5 0.3 pad_maximum_fusion.bias_ref
  4.7 0.8 %copy-done = bf16[512,512]{1,0:T(8,128)(2,1)S(1)} copy-done((bf16[512,512]{1,0:T(8,128)(2,1)S(1)}, bf16[512,512]{1,0:T(8,128)(2,1)}, u32[]{:S(2)}) %copy-start) | copy-done | bytes 524312
  5.5 66.0 %whole.1 = (bf16[16,12,512]{2,1,0:T(8,128)(2,1)S(1)}, bf16[16,12,512]{2,1,0:T(8,128)(2,1)S(1)}, bf16[16,12,512]{2,1,0:T(8,128)(2,1)S(1)}, bf16[512,512]{1,0:T(8,128)(2,1)S(1)}) custom-call(f32[768,384]{1,0:T(8,128)S(1)} %pad_maximum_fusion.bias_ref, bf16[16,12,512]{2,1,0:T(8,128)(2,1)S(1)} %copy.9.queries_ref, bf16[16,12,512]{2,1,0:T(8,128)(2,1)S(1)} %copy.10.keys_ref, ...), custom_call_target="tpu_custom_call" | custom-call | tf_op jit(solution)/shard_map/whole/pallas_call | solution.py:324
  71.5 0.8 %copy.13 = bf16[16,12,512]{2,0,1:T(8,128)(2,1)} copy(bf16[16,12,512]{2,1,0:T(8,128)(2,1)S(1)} %get-tuple-element.4) | data formatting | bytes 393216 | tf_op jit(solution)/shard_map/whole/pallas_call | solution.py:324
  72.3 0.8 %copy.14 = bf16[16,12,512]{2,0,1:T(8,128)(2,1)} copy(bf16[16,12,512]{2,1,0:T(8,128)(2,1)S(1)} %get-tuple-element.5) | data formatting | bytes 393216 | tf_op jit(solution)/shard_map/whole/pallas_call | solution.py:324
  73.0 0.8 %copy.15 = bf16[16,12,512]{2,0,1:T(8,128)(2,1)} copy(bf16[16,12,512]{2,1,0:T(8,128)(2,1)S(1)} %get-tuple-element.6) | data formatting | bytes 393216 | tf_op jit(solution)/shard_map/whole/pallas_call | solution.py:324
  73.8 0.8 %copy.17 = bf16[512,512]{1,0:T(8,128)(2,1)} copy(bf16[512,512]{1,0:T(8,128)(2,1)S(1)} %get-tuple-element.19) | data formatting | bytes 1048576
  (3 shorter events, 0.1 us)
Async XLA Ops:
  0.6 3.2 %copy-start.1 = (bf16[16,12,512]{2,0,1:T(8,128)(2,1)S(1)}, bf16[16,12,512]{2,0,1:T(8,128)(2,1)}, u32[]{:S(2)}) copy-start(bf16[16,12,512]{2,0,1:T(8,128)(2,1)} %param.9) | copy-start | bytes 589828
  4.5 1.0 %copy-start = (bf16[512,512]{1,0:T(8,128)(2,1)S(1)}, bf16[512,512]{1,0:T(8,128)(2,1)}, u32[]{:S(2)}) copy-start(bf16[512,512]{1,0:T(8,128)(2,1)} %w_ref.1) | copy-start | bytes 1572868

commit v6 on v5

--- a/solution.py
+++ b/solution.py
@@ -56,21 +56,21 @@
 
 
 def quad_of(ref, a, b):
-    rows, cols, _ = ref.shape
+    cols, rows, _ = ref.shape
     high, wide = rows // 2, cols // 2
     strips = [
-        ref[a * high + i].astype(jnp.float32)[b * wide : (b + 1) * wide] for i in range(high)
+        ref[b * wide + j].astype(jnp.float32)[a * high : (a + 1) * high] for j in range(wide)
     ]
     return jnp.concatenate(strips, axis=0).astype(jnp.bfloat16)
 
 
 def put_rows(ref, a, west, east, lanes):
-    rows, cols, _ = ref.shape
+    cols, rows, _ = ref.shape
     high, wide = rows // 2, cols // 2
-    for i in range(high):
-        cut = slice(i * wide, (i + 1) * wide)
-        row = jnp.concatenate([west[cut], east[cut]], axis=0)
-        ref[a * high + i, :, lanes] = row.astype(jnp.bfloat16)
+    for b, part in enumerate((west, east)):
+        for j in range(wide):
+            piece = part[j * high : (j + 1) * high].astype(jnp.bfloat16)
+            ref[b * wide + j, a * high : (a + 1) * high, lanes] = piece
 
 
 def whole_kernel(
@@ -289,7 +289,7 @@
     def places(count):
         ids = jnp.arange(count * count * high * wide, dtype=jnp.int32)
         quad, cell = ids // (high * wide), ids % (high * wide)
-        return (quad // count) * high + cell // wide, (quad % count) * wide + cell % wide
+        return (quad // count) * high + cell % high, (quad % count) * wide + cell // high
 
     key_row, key_col = places(4)
     key_row, key_col = key_row - high, key_col - wide
@@ -305,6 +305,10 @@
     return jnp.concatenate([bias, bias], axis=1)
 
 
+def turned(field):
+    return field.transpose(1, 0, 2)
+
+
 def shards(queries, keys, values, out_weight, d_out):
     rows, cols, width = queries.shape
     all_rows = rows * N_LAT
@@ -320,8 +324,8 @@
     lanes = width // pairs
     chunk = width // (2 * N_X)
     high = chunk * pairs // N_Z
-    field = jax.ShapeDtypeStruct((rows, cols, width), bf16)
-    return pl.pallas_call(
+    field = jax.ShapeDtypeStruct((cols, rows, width), bf16)
+    d_queries, d_keys, d_values, d_weight = pl.pallas_call(
         functools.partial(whole_kernel, weight_scale),
         out_shape=(field, field, field, jax.ShapeDtypeStruct((width, width), bf16)),
         in_specs=[VMEM] * 6,
@@ -354,7 +358,8 @@
             collective_id=0, has_side_effects=True, vmem_limit_bytes=48 << 20
         ),
         name="whole",
-    )(bias, queries, keys, values, out_weight, d_out)
+    )(bias, turned(queries), turned(keys), turned(values), out_weight, turned(d_out))
+    return turned(d_queries), turned(d_keys), turned(d_values), d_weight
 
 
 def solution(mesh):

time: 74.9 us -> 71.9 us (0.960)
  local copies, waits for them, and re-layouts: 7.18 us -> 3.79 us
    pallas_call x3 -> x0, local copies, waits for them, and re-layouts: 2.37 us -> none  [shards(): pl.pallas_call(functools.partial(whole_kernel, weight_scale), out_shape=(...]
    unnamed x9 -> x14, local copies, waits for them, and re-layouts: 4.81 us -> 3.79 us
where the time goes in v6:
time: 71.9 us; the launch traced here: 71.7 us
  Pallas kernels  66.5 us (92%)
  local copies, waits for them, and re-layouts  3.79 us (5%)
  other arithmetic  0.79 us (1%)
    pallas_call x1, Pallas kernels, shards(): pl.pallas_call(functools.partial(whole_kernel, weight_scale), out_shape=(...  66.5 us
    unnamed x14, local copies, waits for them, and re-layouts  3.79 us

profile of v6, /device:TPU:1, one launch (start us, length us, event | category | flops | bytes accessed | tf_op | source)
XLA Modules:
  0.0 71.7 jit_solution(9740484247337756478)
XLA Ops:
  0.7 0.5 fusion.2
  1.2 0.0 copy-start
  1.2 0.0 copy-start.1
  1.2 0.0 copy-start.2
  1.2 0.0 copy-start.3
  1.2 0.0 copy-start.4
  1.2 0.3 pad_maximum_fusion.bias_ref
  1.5 0.7 copy-done
  2.2 0.0 copy-done.1
  2.3 0.1 copy-done.2
  2.3 0.1 copy-done.3
  2.4 0.1 copy-done.4
  2.4 66.5 %whole.1 = (bf16[12,16,512]{2,1,0:T(8,128)(2,1)S(1)}, bf16[12,16,512]{2,1,0:T(8,128)(2,1)S(1)}, bf16[12,16,512]{2,1,0:T(8,128)(2,1)S(1)}, bf16[512,512]{1,0:T(8,128)(2,1)S(1)}) custom-call(f32[768,384]{1,0:T(8,128)S(1)} %pad_maximum_fusion.bias_ref, bf16[12,16,512]{2,1,0:T(8,128)(2,1)S(1)} %bitcast.7, bf16[12,16,512]{2,1,0:T(8,128)(2,1)S(1)} %bitcast.8, ...), custom_call_target="tpu_custom_call" | custom-call | tf_op jit(solution)/shard_map/whole/pallas_call | solution.py:328
  68.9 0.7 copy.13
  69.6 0.7 copy.14
  70.3 0.7 copy.15
  70.9 0.8 %copy.16 = bf16[512,512]{1,0:T(8,128)(2,1)} copy(bf16[512,512]{1,0:T(8,128)(2,1)S(1)} %get-tuple-element.23) | data formatting | bytes 1048576
  (3 shorter events, 0.1 us)
Async XLA Ops:
  1.2 1.0 %copy-start = (bf16[512,512]{1,0:T(8,128)(2,1)S(1)}, bf16[512,512]{1,0:T(8,128)(2,1)}, u32[]{:S(2)}) copy-start(bf16[512,512]{1,0:T(8,128)(2,1)} %w_ref.1) | copy-start | bytes 1572868
  1.2 1.1 %copy-start.1 = (bf16[16,12,512]{2,0,1:T(8,128)(2,1)S(1)}, bf16[16,12,512]{2,0,1:T(8,128)(2,1)}, u32[]{:S(2)}) copy-start(bf16[16,12,512]{2,0,1:T(8,128)(2,1)} %param.5) | copy-start | bytes 589828
  1.2 1.1 %copy-start.2 = (bf16[16,12,512]{2,0,1:T(8,128)(2,1)S(1)}, bf16[16,12,512]{2,0,1:T(8,128)(2,1)}, u32[]{:S(2)}) copy-start(bf16[16,12,512]{2,0,1:T(8,128)(2,1)} %param.6) | copy-start | bytes 589828
  1.2 1.2 %copy-start.3 = (bf16[16,12,512]{2,0,1:T(8,128)(2,1)S(1)}, bf16[16,12,512]{2,0,1:T(8,128)(2,1)}, u32[]{:S(2)}) copy-start(bf16[16,12,512]{2,0,1:T(8,128)(2,1)} %param.7) | copy-start | bytes 589828
  1.2 1.2 %copy-start.4 = (bf16[16,12,512]{2,0,1:T(8,128)(2,1)S(1)}, bf16[16,12,512]{2,0,1:T(8,128)(2,1)}, u32[]{:S(2)}) copy-start(bf16[16,12,512]{2,0,1:T(8,128)(2,1)} %param.9) | copy-start | bytes 589828
